TPU v7x, 32 devices: a whole 2x2x4 slice. The times are simulated.
32 devices in a mesh: probe: 16 (over z, y, core), strip: 2 (over x).
Axes of the slice: x: 2, y: 2, z: 4, core: 2. Of those that a mesh axis runs over, the one named last changes fastest.
Arguments:
- potential: float32 [2, 512, 2048], P(None, 'probe', 'strip'), may hold values from 0 to 2
- probe_wave: float32 [2, 256, 256], replicated, may hold values from -6 to 6
- offsets: int32 [2, 2, 96], P('strip'), may hold values from -128 to 896, as said below
- members: int32 [2, 16, 6], P('strip', 'probe'), may hold values from 0 to 95, as said below
- counts: int32 [2, 16], P('strip', 'probe'), may hold values from 1 to 6, as said below
- measured: float32 [2, 16, 6, 256, 256], P('strip', 'probe'), may hold values from 0 to 4
Outputs:
- potential_grad: float32 [2, 512, 2048], P(None, 'probe', 'strip')
Inputs may be any that keep to these rules, and one draw needn't show every extreme that they name: offsets[s, 0, p] is a window's first row, 0 to 256; offsets[s, 1, p] its first column counted from the strip's first column, -128 to 896; both ends of both ranges occur in every strip. `members`: every position of a strip is listed exactly once over that strip's groups; a group uses its first counts[s, g] entries. `counts`: in every strip some group uses all 6 slots and some group uses one.
All inputs are finite; a program needn't handle non-finite values.
Results may differ from a plain program's by a relative error of at most 0.00021.
Values sent between devices are 32-bit elements; how exact they have to be, the bound alone decides.
No kernel may reach another device: no remote copies, remote signals or barrier semaphores. Data moves between devices by JAX's collectives and lax.ppermute only.
A program may use at most 64 MiB of HBM per device.

v0:
```python
import math

import jax
import jax.numpy as jnp
from jax import lax
from jax.sharding import PartitionSpec as P

EDGE = 128


A_PROP = 0.1
LOSS_SCALE = 0.03125


def extended(value, sides, width):
    for axis, dim in sides:
        peers, length = (lax.axis_size(axis), value.shape[dim])
        up = [(i, (i + 1) % peers) for i in range(peers - 1)]
        down = [(j, i) for i, j in up]
        last = lax.slice_in_dim(value, length - width, length, axis=dim)
        initial = lax.slice_in_dim(value, 0, width, axis=dim)
        before = lax.ppermute(last, axis, up)
        after = lax.ppermute(initial, axis, down)
        value = jnp.concatenate([before, value, after], axis=dim)
    return value


def laplace(values):
    padded = jnp.pad(values, ((1, 1), (1, 1)))
    return (
        padded[2:, 1:-1] + padded[:-2, 1:-1] + padded[1:-1, 2:] + padded[1:-1, :-2] - 4.0 * values
    )


def propagate(real_part, imag_part):
    term_re, term_im = (real_part, imag_part)
    out_re, out_im = (real_part, imag_part)
    for degree in range(1, 5):
        lap_re = laplace(term_re)
        lap_im = laplace(term_im)
        term_re, term_im = (-A_PROP / degree * lap_im, A_PROP / degree * lap_re)
        out_re = out_re + term_re
        out_im = out_im + term_im
    return (out_re, out_im)


def exit_wave(window, probe_wave):
    real_part, imag_part = (probe_wave[0], probe_wave[1])
    for slice_index in range(window.shape[0]):
        phases = window[slice_index]
        cosine, sine_part = (jnp.cos(phases), jnp.sin(phases))
        real_part, imag_part = (
            real_part * cosine - imag_part * sine_part,
            real_part * sine_part + imag_part * cosine,
        )
        real_part, imag_part = propagate(real_part, imag_part)
    return (real_part, imag_part)


def dft_tables(window_size):
    indices = jnp.arange(window_size, dtype=jnp.int32)
    product = indices[:, None] * indices[None, :] % window_size
    angles = -2.0 * math.pi / window_size * product.astype(jnp.float32)
    normal_scale = 1.0 / math.sqrt(window_size)
    return (jnp.cos(angles) * normal_scale, jnp.sin(angles) * normal_scale)


def matmul(left_side, right_side):
    return jnp.dot(
        left_side, right_side, precision=lax.Precision.HIGHEST, preferred_element_type=jnp.float32
    )


def slot_loss(window, probe_wave, intensity_data, table_re, table_im):
    real_part, imag_part = exit_wave(window, probe_wave)
    inner_re = matmul(table_re, real_part) - matmul(table_im, imag_part)
    inner_im = matmul(table_re, imag_part) + matmul(table_im, real_part)
    far_re = matmul(inner_re, table_re) - matmul(inner_im, table_im)
    far_im = matmul(inner_re, table_im) + matmul(inner_im, table_re)
    intensity = far_re * far_re + far_im * far_im
    return LOSS_SCALE * jnp.sum((intensity - intensity_data) ** 2)


def split_edges(gradient, own_width):
    outgoing = jnp.concatenate([gradient[:, :, :EDGE], gradient[:, :, own_width + EDGE :]], axis=2)
    return (outgoing, gradient[:, :, EDGE : EDGE + own_width])


def add_edges(own_part, arrived, own_width):
    own_part = own_part.at[:, :, :EDGE].add(arrived[:, :, :EDGE])
    return own_part.at[:, :, own_width - EDGE :].add(arrived[:, :, 3 * EDGE :])


def shards(potential, probe_wave, offsets, members, counts, measured):
    own_width = potential.shape[2]
    widened = extended(potential, (("strip", 2),), EDGE)
    whole_object = lax.all_gather(widened, "probe", axis=1, tiled=True)
    window_size = probe_wave.shape[-1]
    table_re, table_im = dft_tables(window_size)
    anchor = jnp.zeros((), jnp.int32)
    loss_grad = jax.grad(slot_loss)

    def visit(slot_index, gradient):
        position = members[0, 0, slot_index]
        start_row = offsets[0, 0, position]
        start_column = offsets[0, 1, position] + EDGE
        window = lax.dynamic_slice(
            whole_object,
            (anchor, start_row, start_column),
            (whole_object.shape[0], window_size, window_size),
        )
        window_grad = loss_grad(window, probe_wave, measured[0, 0, slot_index], table_re, table_im)
        current = lax.dynamic_slice(gradient, (anchor, start_row, start_column), window.shape)
        return lax.dynamic_update_slice(
            gradient, current + window_grad, (anchor, start_row, start_column)
        )

    gradient = lax.fori_loop(0, counts[0, 0], visit, jnp.zeros(whole_object.shape, jnp.float32))
    outgoing, own_part = split_edges(gradient, own_width)
    arrived = extended(outgoing, (("strip", 2),), EDGE)
    folded = add_edges(own_part, arrived, own_width)
    return lax.psum_scatter(folded, "probe", scatter_dimension=1, tiled=True)


def solution(mesh):
    placed = (
        P(None, "probe", "strip"),
        P(),
        P("strip", None, None),
        P("strip", "probe", None),
        P("strip", "probe"),
        P("strip", "probe", None, None, None),
    )
    return jax.shard_map(
        shards, mesh=mesh, in_specs=placed, out_specs=P(None, "probe", "strip"), check_vma=False
    )
```

profile of v0, /device:TPU:0, one launch (start us, length us, event | category | flops | bytes accessed | tf_op | source)
XLA Modules:
  0.0 484.0 jit_solution(17927370276558367795)
XLA Ops:
  7.3 4.9 %collective-permute-start = (f32[2,32,128]{2,1,0:T(8,128)S(1)}, f32[2,32,128]{2,1,0:T(8,128)S(1)}, u32[]{:S(2)}, u32[]{:S(2)}) collective-permute-start(f32[2,32,128]{2,1,0:T(8,128)S(1)} %get-tuple-element.418), channel_id=1, source_target_pairs={{0,1},{2,3},{4,5},{6,7},{8,9},{10,11},{12,13},{14,15},{16,17},{18,... | collective-permute-start | bytes 98312 | tf_op jit(solution)/shard_map/ppermute | solution.py:22
  13.8 4.2 collective-permute-done.1
  21.3 54.9 %all-gather.2.cloned.1.call-done = f32[2,512,1280]{2,0,1:T(2,128)} async-done(((f32[2,32,1280]{2,0,1:T(2,128)}), f32[2,512,1280]{2,0,1:T(2,128)}) %all-gather.2.cloned.1.call-update) | async-done | bytes 5242896 | tf_op jit(solution)/shard_map/all_gather | solution.py:97
  76.2 2.7 broadcast_in_dim.28.clone
  79.0 102.8 %while.17 = (s32[]{:T(128)}, f32[2,512,1280]{2,1,0:T(8,128)}, s32[]{:T(128)}, s32[1,1,6]{2,1,0:T(1,128)S(1)}, s32[1,2,96]{2,1,0:T(2,128)S(1)}, /*index=5*/f32[2,...) while((s32[]{:T(128)}, f32[2,512,1280]{2,1,0:T(8,128)}, ...), condition=%wide.region_1.2_spmd.clone.clone, body=%wide.region_0.1_spmd.clone.clone.sunk | while | flops 3259498496 | bytes 60293496 | solution.py:118
  85.9 2.6 fusion.321
  102.8 1.5 fusion.330
  105.8 2.5 add_multiply_fusion.3
  116.7 1.5 broadcast_multiply_fusion.41
  118.2 1.5 fusion.337
  123.7 6.2 %dynamic_update_slice.10 = f32[2,512,1280]{2,1,0:T(8,128)} dynamic-update-slice(f32[2,512,1280]{2,1,0:T(8,128)} %get-tuple-element.599, f32[2,256,256]{2,1,0:T(8,128)S(1)} %copy.35, s32[]{:T(128)} %constant.243.clone.1..sunk, s32[]{:T(128)S(6)} %select_n.157, s32[]{:T(128)S(6)} %select_n.158) | dynamic-update-slice | bytes 1048580 | tf_op jit(solution)/shard_map/while/body/dynamic_update_slice | solution.py:114
  136.7 2.6 fusion.321
  153.7 1.5 fusion.330
  156.7 2.5 add_multiply_fusion.3
  164.6 1.5 fusion.336
  167.6 1.5 broadcast_multiply_fusion.41
  169.1 1.5 fusion.337
  174.5 6.6 %dynamic_update_slice.10 = f32[2,512,1280]{2,1,0:T(8,128)} dynamic-update-slice(f32[2,512,1280]{2,1,0:T(8,128)} %get-tuple-element.599, f32[2,256,256]{2,1,0:T(8,128)S(1)} %copy.35, s32[]{:T(128)} %constant.243.clone.1..sunk, s32[]{:T(128)S(6)} %select_n.157, s32[]{:T(128)S(6)} %select_n.158) | dynamic-update-slice | bytes 1048580 | tf_op jit(solution)/shard_map/while/body/dynamic_update_slice | solution.py:114
  183.1 208.2 %collective-permute-start.2 = (f32[2,512,128]{2,1,0:T(8,128)S(1)}, f32[2,512,128]{2,1,0:T(8,128)S(1)}, u32[]{:S(2)}, u32[]{:S(2)}) collective-permute-start(f32[2,512,128]{2,1,0:T(8,128)S(1)} %get-tuple-element.417), channel_id=1, source_target_pairs={{0,1},{2,3},{4,5},{6,7},{8,9},{10,11},{12,13},{14,15},{16,17},{18,... | collective-permute-start | bytes 1572872 | tf_op jit(solution)/shard_map/ppermute | solution.py:22
  392.6 4.7 slice.622
  398.0 2.0 add_dynamic-update-slice_fusion
  399.9 2.5 collective-permute-done.3
  402.4 2.0 fusion.229
  404.4 72.8 %reduce-scatter.2.cloned.1.call-done = f32[2,32,1024]{2,1,0:T(8,128)} async-done(((f32[2,512,1024]{2,1,0:T(8,128)}), f32[2,32,1024]{2,1,0:T(8,128)}) %reduce-scatter.2.cloned.1.call-update) | async-done | bytes 262160 | tf_op jit(solution)/shard_map/reduce_scatter | solution.py:122
  (114 shorter events, 65.7 us)
Async XLA Ops:
  6.5 72.4 %copy-start.1 = (s32[1,1,6]{2,1,0:T(1,128)S(1)}, s32[1,1,6]{2,1,0:T(1,128)}, u32[]{:S(2)}) copy-start(s32[1,1,6]{2,1,0:T(1,128)} %param.15) | copy-start | bytes 76
  6.5 72.4 %copy-start = (s32[1,2,96]{2,1,0:T(2,128)S(1)}, s32[1,2,96]{2,1,0:T(2,128)}, u32[]{:S(2)}) copy-start(s32[1,2,96]{2,1,0:T(2,128)} %param.14) | copy-start | bytes 2308
  6.5 69.7 %all-gather.2.cloned.1.call-start = ((), (), s32[]{:S(2)}) async-start(), calls=%async_computation.1 | async-start | bytes 5570560 | tf_op jit(solution)/shard_map/all_gather | solution.py:97
  7.3 6.4 %collective-permute-start = (f32[2,32,128]{2,1,0:T(8,128)S(1)}, f32[2,32,128]{2,1,0:T(8,128)S(1)}, u32[]{:S(2)}, u32[]{:S(2)}) collective-permute-start(f32[2,32,128]{2,1,0:T(8,128)S(1)} %get-tuple-element.418), channel_id=1, source_target_pairs={{0,1},{2,3},{4,5},{6,7},{8,9},{10,11},{12,13},{14,15},{16,17},{18,... | collective-permute-start | bytes 98312 | tf_op jit(solution)/shard_map/ppermute | solution.py:22
  12.2 5.8 %collective-permute-start.1 = (f32[2,32,128]{2,1,0:T(8,128)S(1)}, f32[2,32,128]{2,1,0:T(8,128)S(1)}, u32[]{:S(2)}, u32[]{:S(2)}) collective-permute-start(f32[2,32,128]{2,1,0:T(8,128)S(1)} %get-tuple-element.419), channel_id=1, source_target_pairs={{1,0},{3,2},{5,4},{7,6},{9,8},{11,10},{13,12},{15,14},{17,16},{19,... | collective-permute-start | bytes 98312 | tf_op jit(solution)/shard_map/ppermute | solution.py:23
  20.0 457.1 %reduce-scatter.2.cloned.1.call-start = ((), (), s32[]{:S(2)}) async-start(), calls=%async_computation.2 | async-start | bytes 4456448 | tf_op jit(solution)/shard_map/reduce_scatter | solution.py:122
  183.1 214.9 %collective-permute-start.2 = (f32[2,512,128]{2,1,0:T(8,128)S(1)}, f32[2,512,128]{2,1,0:T(8,128)S(1)}, u32[]{:S(2)}, u32[]{:S(2)}) collective-permute-start(f32[2,512,128]{2,1,0:T(8,128)S(1)} %get-tuple-element.417), channel_id=1, source_target_pairs={{0,1},{2,3},{4,5},{6,7},{8,9},{10,11},{12,13},{14,15},{16,17},{18,... | collective-permute-start | bytes 1572872 | tf_op jit(solution)/shard_map/ppermute | solution.py:22
  391.3 11.1 %collective-permute-start.3 = (f32[2,512,128]{2,1,0:T(8,128)S(1)}, f32[2,512,128]{2,1,0:T(8,128)S(1)}, u32[]{:S(2)}, u32[]{:S(2)}) collective-permute-start(f32[2,512,128]{2,1,0:T(8,128)S(1)} %get-tuple-element.416), channel_id=1, source_target_pairs={{1,0},{3,2},{5,4},{7,6},{9,8},{11,10},{13,12},{15,14},{17,16},{19,... | collective-permute-start | bytes 1572872 | tf_op jit(solution)/shard_map/ppermute | solution.py:23
Sparse Core Ops, SparseCore 0:
  20.1 56.0 all-gather.1
  404.5 72.5 reduce-scatter.1
where the time goes:
time: 487 us; the launch traced here: 484 us
  starting transfers between devices  216 us (44%)
  waiting for transfers between devices  135 us (28%)
  matrix products  47.6 us (10%)
  local copies, waits for them, and re-layouts  40.2 us (8%)
  other arithmetic  19.1 us (4%)
  between operations  13.5 us (3%)
  loops' own time  12.7 us (3%)
    ppermute x2, starting transfers between devices, extended(): before = lax.ppermute(last, axis, up)  213 us
    reduce_scatter x1, waiting for transfers between devices, shards(): return lax.psum_scatter(folded, 'probe', scatter_dimension=1, tiled=True)  72.8 us
    all_gather x1, waiting for transfers between devices, shards(): whole_object = lax.all_gather(widened, 'probe', axis=1, tiled=True)  54.9 us
    dot_general x32, matrix products, matmul(): jnp.dot(left_side, right_side, precision=lax.Precision.HIGHEST, preferred...  47.6 us
    dynamic_update_slice x4, local copies, waits for them, and re-layouts, visit(): lax.dynamic_update_slice(gradient, current + window_grad, (anchor, start_...  13.2 us
    another operation x1, loops' own time, shards(): lax.fori_loop(0, counts[0, 0], visit, jnp.zeros(whole_object.shape, jnp.f...  12.7 us
    mul x40, other arithmetic, propagate(): term_re, term_im = (-A_PROP / degree * lap_im, A_PROP / degree * lap_re)  9.92 us
  transfers between devices with their start and end apart: 6, of which 6 were waited for; matrix products, arithmetic and copies ran while one was open for 2% of the time, Pallas kernels for 0%

commit v1 on v0

v1 whole, which is shorter than its diff:
```python
import math

import jax
import jax.numpy as jnp
from jax import lax
from jax.experimental import pallas as pl
from jax.experimental.pallas import tpu as pltpu
from jax.sharding import PartitionSpec as P

EDGE = 128
A_PROP = 0.1
LOSS_SCALE = 0.03125
LANES = 128
SUB = 8
COS = (0.9999999993567104, -0.4999999690796125, 0.041666428711172335, -0.0013882473076505886, 2.4093931432702378e-05)
SIN = (0.9999999999413409, -0.1666666638472293, 0.008333311638477454, -0.00019835422091007726, 2.6912728384156356e-06)


def extended(value, sides, width):
    for axis, dim in sides:
        peers, length = (lax.axis_size(axis), value.shape[dim])
        up = [(i, (i + 1) % peers) for i in range(peers - 1)]
        down = [(j, i) for i, j in up]
        last = lax.slice_in_dim(value, length - width, length, axis=dim)
        initial = lax.slice_in_dim(value, 0, width, axis=dim)
        before = lax.ppermute(last, axis, up)
        after = lax.ppermute(initial, axis, down)
        value = jnp.concatenate([before, value, after], axis=dim)
    return value


def split(value):
    high = value.astype(jnp.bfloat16)
    return high, (value - high.astype(jnp.float32)).astype(jnp.bfloat16)


def split_table(value):
    high = lax.reduce_precision(value, 8, 7)
    return high.astype(jnp.bfloat16), (value - high).astype(jnp.bfloat16)


def tables(size):
    groups = size // SUB
    indices = jnp.arange(size, dtype=jnp.int32)
    order = indices % SUB * groups + indices // SUB

    def wave(rows, columns):
        angles = -2.0 * math.pi / size * (rows[:, None] * columns[None, :] % size).astype(jnp.float32)
        scale = 1.0 / math.sqrt(size)
        return jnp.cos(angles) * scale, jnp.sin(angles) * scale

    def left(real, imag):
        full = jnp.concatenate([jnp.concatenate([real, -imag], 1), jnp.concatenate([imag, real], 1)], 0)
        high, low = split_table(full)
        return jnp.concatenate([high, high, low], 1)

    def right(real, imag):
        full = jnp.concatenate([jnp.concatenate([real, imag], 1), jnp.concatenate([-imag, real], 1)], 0)
        high, low = split_table(full)
        return jnp.concatenate([high, high, low], 0)

    forward = wave(indices, order)
    backward = wave(order, indices)
    return left(*forward), left(*backward), right(*wave(indices, indices))


def kernel(
    rows_ref, columns_ref, count_ref,
    object_ref, probe_ref, measured_ref, left_ref, left_back_ref, right_ref,
    out_ref,
    base, ping, pong, first, second, turn, stack, wide,
    *, height, blocks, slices,
):
    slot = pl.program_id(0)
    size = measured_ref.shape[-1]
    groups = size // SUB
    halves = size // LANES
    per_block = blocks * slices * height
    stride = groups // height * per_block
    lane = lax.broadcasted_iota(jnp.int32, (SUB, LANES), 1)
    sub = lax.broadcasted_iota(jnp.int32, (SUB, LANES), 0)

    @pl.when(slot == 0)
    def _():
        def clear(i, carry):
            out_ref[pl.ds(pl.multiple_of(i * LANES, LANES), LANES), :] = jnp.zeros((LANES, LANES), jnp.float32)
            return carry
        lax.fori_loop(0, out_ref.shape[0] // LANES, clear, 0)

    @pl.when(slot < count_ref[0])
    def _():
        start_row = rows_ref[slot]
        start_column = columns_ref[slot]
        block = start_column // LANES
        shift = start_column % LANES
        back = lax.rem(LANES - shift, LANES)
        places = [jnp.minimum(block + k, blocks - 1) * (slices * height) for k in range(halves + 1)]
        keep = lane < LANES - shift
        spill = lane < shift

        def object_rows(t, j):
            at = start_row + t
            return at // height * per_block + j * height + at % height

        def window(t, j):
            top = object_rows(t, j)
            parts = [pltpu.roll(object_ref[pl.ds(top + c, SUB, stride=stride), :], back, 1) for c in places]
            return [jnp.where(keep, parts[k], parts[k + 1]) for k in range(halves)]

        def phase(t, j):
            out = []
            for value in window(t, j):
                theta = value - 1.0
                z = theta * theta
                c = COS[4]
                s = SIN[4]
                for k in (3, 2, 1, 0):
                    c = c * z + COS[k]
                    s = s * z + SIN[k]
                out.append((c, s * theta))
            return out

        def tile(t):
            return pl.ds(pl.multiple_of((t + 1) * SUB, SUB), SUB)

        def half(h):
            return pl.ds(h * LANES, LANES)

        def halo(ref):
            for part in range(2):
                for h in range(halves):
                    bottom = ref[part, tile(groups - 1), half(h)]
                    top = ref[part, tile(0), half(h)]
                    ref[part, tile(-1), half(h)] = jnp.where(sub == 0, 0.0, pltpu.roll(bottom, 1, 0))
                    ref[part, tile(groups), half(h)] = jnp.where(sub == SUB - 1, 0.0, pltpu.roll(top, SUB - 1, 0))

        def laplace(ref, part, t):
            out = []
            middle = [ref[part, tile(t), half(h)] for h in range(halves)]
            right_rolled = [pltpu.roll(v, 1, 1) for v in middle]
            left_rolled = [pltpu.roll(v, LANES - 1, 1) for v in middle]
            for h in range(halves):
                before = jnp.where(lane == 0, right_rolled[h - 1] if h else 0.0, right_rolled[h])
                after = jnp.where(lane == LANES - 1, left_rolled[h + 1] if h + 1 < halves else 0.0, left_rolled[h])
                around = (before + after) + (ref[part, tile(t - 1), half(h)] + ref[part, tile(t + 1), half(h)])
                out.append(around - 4.0 * middle[h])
            return out

        def step(src, dst, factor):
            def body(i, carry):
                for d in range(4):
                    t = i * 4 + d
                    lap_re = laplace(src, 0, t)
                    lap_im = laplace(src, 1, t)
                    for h in range(halves):
                        dst[0, tile(t), half(h)] = base[0, tile(t), half(h)] - factor * lap_im[h]
                        dst[1, tile(t), half(h)] = base[1, tile(t), half(h)] + factor * lap_re[h]
                return carry
            lax.fori_loop(0, groups // 4, body, 0)

        def propagate():
            halo(base)
            step(base, ping, A_PROP / 4)
            halo(ping)
            step(ping, pong, A_PROP / 3)
            halo(pong)
            step(pong, ping, A_PROP / 2)
            halo(ping)
            step(ping, pong, A_PROP)

        def each(body):
            def run(i, carry):
                for d in range(4):
                    body(i * 4 + d)
                return carry
            lax.fori_loop(0, groups // 4, run, 0)

        def enter_first(t):
            for h, (c, s) in enumerate(phase(t, 0)):
                re = probe_ref[pl.ds(h * size + t, SUB, stride=groups), :]
                im = probe_ref[pl.ds((halves + h) * size + t, SUB, stride=groups), :]
                new_re, new_im = re * c - im * s, re * s + im * c
                base[0, tile(t), half(h)] = new_re
                base[1, tile(t), half(h)] = new_im
                first[0, tile(t), half(h)] = new_re
                first[1, tile(t), half(h)] = new_im

        def enter_second(t):
            for h, (c, s) in enumerate(phase(t, 1)):
                re = pong[0, tile(t), half(h)]
                im = pong[1, tile(t), half(h)]
                new_re, new_im = re * c - im * s, re * s + im * c
                base[0, tile(t), half(h)] = new_re
                base[1, tile(t), half(h)] = new_im
                second[0, tile(t), half(h)] = new_re
                second[1, tile(t), half(h)] = new_im
                turn[0, tile(t), half(h)] = c
                turn[1, tile(t), half(h)] = s

        def add_gradient(t, j, grads):
            top = object_rows(t, j)
            rolled = [pltpu.roll(g, shift, 1) for g in grads]
            for k, c in enumerate(places):
                here = jnp.where(spill, rolled[k - 1] if k else 0.0, rolled[k] if k < halves else 0.0)
                rows = pl.ds(top + c, SUB, stride=stride)
                out_ref[rows, :] = out_ref[rows, :] + here

        def leave_second(t):
            grads = []
            for h in range(halves):
                re = pong[0, tile(t), half(h)]
                im = pong[1, tile(t), half(h)]
                grads.append(-(re * second[1, tile(t), half(h)] + im * second[0, tile(t), half(h)]))
                c = turn[0, tile(t), half(h)]
                s = turn[1, tile(t), half(h)]
                base[0, tile(t), half(h)] = re * c - im * s
                base[1, tile(t), half(h)] = re * s + im * c
            add_gradient(t, 1, grads)

        def leave_first(t):
            grads = []
            for h in range(halves):
                re = pong[0, tile(t), half(h)]
                im = pong[1, tile(t), half(h)]
                grads.append(-(re * first[1, tile(t), half(h)] + im * first[0, tile(t), half(h)]))
            add_gradient(t, 0, grads)

        def dot(a, b):
            return jnp.dot(a, b, preferred_element_type=jnp.float32)

        def put_wide(real, imag):
            for k, value in enumerate((real, imag)):
                high, low = split(value)
                for place, piece in ((k, high), (2 + k, low), (4 + k, high)):
                    wide[:, place * size:(place + 1) * size] = piece

        each(enter_first)
        propagate()
        each(enter_second)
        propagate()
        for part in range(2):
            high, low = split(pong[part, SUB:SUB + size, :])
            for place, piece in ((part, high), (2 + part, low), (4 + part, high)):
                stack[place * size:(place + 1) * size, :] = piece
        inner = dot(left_ref[...], stack[...])
        put_wide(inner[:size], inner[size:])
        far = dot(wide[...], right_ref[...])
        far_re, far_im = far[:, :size], far[:, size:]
        scaled = (4.0 * LOSS_SCALE) * ((far_re * far_re + far_im * far_im) - measured_ref[...])
        put_wide(scaled * far_re, -(scaled * far_im))
        inner = dot(wide[...], right_ref[...])
        for part in range(2):
            high, low = split(inner[:, part * size:(part + 1) * size])
            for place, piece in ((part, high), (2 + part, low), (4 + part, high)):
                stack[place * size:(place + 1) * size, :] = piece
        outer = dot(left_back_ref[...], stack[...])
        base[0, SUB:SUB + size, :] = outer[:size]
        base[1, SUB:SUB + size, :] = outer[size:]
        propagate()
        each(leave_second)
        propagate()
        each(leave_first)


def window_gradients(rows, columns, count, whole, probe, measured, height, slices):
    size = measured.shape[-1]
    slots = measured.shape[0]
    padded = size + 2 * SUB
    blocks = whole.shape[1] // (slices * height)
    peers = whole.shape[0]
    whole = whole.reshape(-1, LANES)
    left, left_back, right = tables(size)
    full = lambda a: pl.BlockSpec(a.shape, lambda k, *_: (0,) * a.ndim)
    field = pltpu.VMEM((2, padded, size), jnp.float32)
    return pl.pallas_call(
        lambda *refs: kernel(*refs, height=height, blocks=blocks, slices=slices),
        grid_spec=pltpu.PrefetchScalarGridSpec(
            num_scalar_prefetch=3,
            grid=(slots,),
            in_specs=[
                full(whole), full(probe),
                pl.BlockSpec((None, size, size), lambda k, *_: (k, 0, 0)),
                full(left), full(left_back), full(right),
            ],
            out_specs=pl.BlockSpec(whole.shape, lambda k, *_: (0, 0)),
            scratch_shapes=[field] * 6 + [
                pltpu.VMEM((6 * size, size), jnp.bfloat16),
                pltpu.VMEM((size, 6 * size), jnp.bfloat16),
            ],
        ),
        out_shape=jax.ShapeDtypeStruct(whole.shape, jnp.float32),
        compiler_params=pltpu.CompilerParams(vmem_limit_bytes=56 * 2**20),
        name="windows",
    )(rows, columns, count, whole, probe, measured, left, left_back, right)


def to_blocks(value):
    slices, height, width = value.shape
    return value.reshape(slices * height, width // LANES, LANES).transpose(1, 0, 2)


def from_blocks(value, slices):
    blocks, rows, lanes = value.shape
    return value.transpose(1, 0, 2).reshape(slices, rows // slices, blocks * lanes)


def shards(potential, probe_wave, offsets, members, counts, measured):
    slices, height, own_width = potential.shape
    size = probe_wave.shape[-1]
    strips = lax.axis_size("strip")
    up = [(i, i + 1) for i in range(strips - 1)]
    down = [(j, i) for i, j in up]
    own = to_blocks(potential)
    edge = EDGE // LANES
    from_left = lax.ppermute(own[-edge:], "strip", up)
    from_right = lax.ppermute(own[:edge], "strip", down)
    widened = jnp.concatenate([from_left, own, from_right], 0).reshape(-1, LANES)
    gathered = lax.all_gather(widened, "probe", axis=0, tiled=False)
    positions = members[0, 0]
    rows = offsets[0, 0][positions]
    columns = offsets[0, 1][positions] + EDGE
    probe = probe_wave.reshape(2 * size, size // LANES, LANES)
    probe = probe.reshape(2, size, size // LANES, LANES).transpose(0, 2, 1, 3).reshape(-1, LANES)
    gradient = window_gradients(rows, columns, counts[0], gathered, probe, measured[0, 0], height, slices)
    mine = lax.psum_scatter(gradient.reshape(gathered.shape), "probe", scatter_dimension=0, tiled=False)
    mine = mine.reshape(-1, slices * height, LANES)
    from_left = lax.ppermute(mine[-edge:], "strip", up)
    from_right = lax.ppermute(mine[:edge], "strip", down)
    middle = mine[edge:-edge]
    middle = middle.at[:edge].add(from_left).at[-edge:].add(from_right)
    return from_blocks(middle, slices)


def solution(mesh):
    placed = (
        P(None, "probe", "strip"),
        P(),
        P("strip", None, None),
        P("strip", "probe", None),
        P("strip", "probe"),
        P("strip", "probe", None, None, None),
    )
    return jax.shard_map(
        shards, mesh=mesh, in_specs=placed, out_specs=P(None, "probe", "strip"), check_vma=False
    )
```

time: 487 us -> 311 us (0.64)
  starting transfers between devices: 216 us -> 10.9 us
  Pallas kernels: 0 us -> 141 us
  matrix products: 47.6 us -> 0 us
  local copies, waits for them, and re-layouts: 40.2 us -> 7.18 us
  loops' own time: 12.7 us -> 0 us
  waiting for transfers between devices: 135 us -> 127 us
  other arithmetic: 19.1 us -> 11.3 us
    ppermute x4, starting transfers between devices: 216 us -> 10.8 us  [the longest x1 4.87 us: shards(): from_left = lax.ppermute(own[-edge:], 'strip', up)]
    pallas_call x0 -> x1, Pallas kernels: none -> 141 us  [window_gradients(): pl.pallas_call(lambda *refs: kernel(*refs, height=height, blocks=blocks,...]
    dot_general x32 -> x0, matrix products: 47.6 us -> none  [matmul(): jnp.dot(left_side, right_side, precision=lax.Precision.HIGHEST, preferred...]
    dynamic_update_slice x4 -> x0, local copies, waits for them, and re-layouts: 13.2 us -> none  [visit(): lax.dynamic_update_slice(gradient, current + window_grad, (anchor, start_...]
    another operation x1 -> x0, loops' own time: 12.7 us -> none  [shards(): lax.fori_loop(0, counts[0, 0], visit, jnp.zeros(whole_object.shape, jnp.f...]
    all_gather x1, waiting for transfers between devices: 54.9 us -> 42.3 us  [shards(): gathered = lax.all_gather(widened, 'probe', axis=0, tiled=False)]
    slice x5 -> x3, local copies, waits for them, and re-layouts: 12 us -> 1.76 us  [the longest x1 0.97 us: shards(): middle = mine[edge:-edge]]
    mul x40 -> x1, other arithmetic: 9.92 us -> 1.06 us  [wave(): return (jnp.cos(angles) * scale, jnp.sin(angles) * scale)]
  transfers between devices with their start and end apart: 6 -> 6, of which waited for: 6 -> 5; matrix products, arithmetic and copies ran while one was open for 2% -> 5% of each run, Pallas kernels for 0% -> 0%
where the time goes in v1:
time: 311 us
  Pallas kernels  141 us (45%)
  waiting for transfers between devices  127 us (41%)
  between operations  14.1 us (5%)
  other arithmetic  11.3 us (4%)
  starting transfers between devices  10.9 us (4%)
  local copies, waits for them, and re-layouts  7.18 us (2%)
    pallas_call x1, Pallas kernels, window_gradients(): pl.pallas_call(lambda *refs: kernel(*refs, height=height, blocks=blocks,...  141 us
    reduce_scatter x1, waiting for transfers between devices, shards(): lax.psum_scatter(gradient.reshape(gathered.shape), 'probe', scatter_dimen...  77.2 us
    all_gather x1, waiting for transfers between devices, shards(): gathered = lax.all_gather(widened, 'probe', axis=0, tiled=False)  42.3 us
  transfers between devices with their start and end apart: 6, of which 5 were waited for; matrix products, arithmetic and copies ran while one was open for 5% of the time, Pallas kernels for 0%

profile of v1, /device:TPU:0, one launch (start us, length us, event | category | flops | bytes accessed | tf_op | source)
XLA Modules:
  0.0 311.0 jit_solution(7688935225095987237)
XLA Ops:
  6.5 1.1 copy.17
  7.7 4.9 %collective-permute-start = (f32[1,64,128]{2,1,0:T(8,128)S(1)}, f32[1,64,128]{2,1,0:T(8,128)S(1)}, u32[]{:S(2)}, u32[]{:S(2)}) collective-permute-start(f32[1,64,128]{2,1,0:T(8,128)S(1)} %get-tuple-element.37), channel_id=1, source_target_pairs={{0,1},{2,3},{4,5},{6,7},{8,9},{10,11},{12,13},{14,15},{16,17},{18,... | collective-permute-start | bytes 98312 | tf_op jit(solution)/shard_map/ppermute | solution.py:315
  12.6 1.3 collective-permute-start.1
  14.1 4.2 %collective-permute-done.1 = f32[1,64,128]{2,1,0:T(8,128)S(1)} collective-permute-done((f32[1,64,128]{2,1,0:T(8,128)S(1)}, f32[1,64,128]{2,1,0:T(8,128)S(1)}, u32[]{:S(2)}, u32[]{:S(2)}) %collective-permute-start.1) | collective-permute-done | bytes 32800 | tf_op jit(solution)/shard_map/ppermute | solution.py:316
  18.4 0.8 pad_maximum_fusion.3
  20.5 0.8 slice_bitcast_fusion
  21.9 1.2 gather_fusion
  23.1 1.0 fusion.21
  24.1 1.1 sine_multiply_fusion
  25.3 2.2 fusion.23
  28.3 0.9 copy_bitcast_fusion
  29.2 1.3 pad_maximum_fusion.2.refs_8_
  30.5 1.3 pad_maximum_fusion.1.refs_7_
  31.8 1.2 pad_maximum_fusion.refs_6_
  33.0 42.3 %all-gather.2.cloned.1.call-done = f32[16,640,128]{2,1,0:T(8,128)} async-done(((f32[1,640,128]{2,1,0:T(8,128)}), f32[16,640,128]{2,1,0:T(8,128)}) %all-gather.2.cloned.1.call-update) | async-done | bytes 5242896 | tf_op jit(solution)/shard_map/all_gather | solution.py:318
  75.4 140.7 %windows.1 = f32[10240,128]{1,0:T(8,128)} custom-call(s32[6]{0:T(128)} %gather_fusion, s32[6]{0:T(128)} %broadcast_add_fusion.refs_1_, s32[1]{0:T(128)} %bitcast.29.refs_2_, f32[10240,128]{1,0:T(8,128)} %bitcast.31, f32[1024,128]{1,0:T(8,128)} %bitcast.32, f32[6,256,256]{2,1,0:T(8,128)} %bitcast.33, bf16[512,1536]{1,0:T(8,128)(2,1)} %pad_maximum_fusion.refs_6_, ...), custom_call_target="tpu_custom_call" | custom-call | tf_op jit(solution)/shard_map/windows/pallas_call | solution.py:275
  216.1 77.2 %reduce-scatter.2.cloned.1.call-done = f32[1,640,128]{2,1,0:T(8,128)} async-done(((f32[16,640,128]{2,1,0:T(8,128)}), f32[1,640,128]{2,1,0:T(8,128)}) %reduce-scatter.2.cloned.1.call-update) | async-done | bytes 327696 | tf_op jit(solution)/shard_map/reduce_scatter | solution.py:325
  293.3 0.8 fusion.31
  294.0 3.4 %collective-permute-start.2 = (f32[1,64,128]{2,1,0:T(8,128)S(1)}, f32[1,64,128]{2,1,0:T(8,128)S(1)}, u32[]{:S(2)}, u32[]{:S(2)}) collective-permute-start(f32[1,64,128]{2,1,0:T(8,128)S(1)} %get-tuple-element.36), channel_id=1, source_target_pairs={{0,1},{2,3},{4,5},{6,7},{8,9},{10,11},{12,13},{14,15},{16,17},{18,... | collective-permute-start | bytes 98312 | tf_op jit(solution)/shard_map/ppermute | solution.py:327
  297.4 1.3 collective-permute-start.3
  298.7 1.0 slice.92
  299.7 0.8 fusion.25
  300.5 2.8 collective-permute-done.3
  303.4 0.7 reshape.155
  (19 shorter events, 2.9 us)
Async XLA Ops:
  6.5 21.8 %copy-start = (f32[2,256,256]{2,1,0:T(8,128)S(1)}, f32[2,256,256]{2,1,0:T(8,128)}, u32[]{:S(2)}) copy-start(f32[2,256,256]{2,1,0:T(8,128)} %param.11) | copy-start | bytes 1572868
  6.5 68.8 %all-gather.2.cloned.1.call-start = ((), (), s32[]{:S(2)}) async-start(), calls=%async_computation.1 | async-start | bytes 5570560 | tf_op jit(solution)/shard_map/all_gather | solution.py:318
  7.7 6.5 %collective-permute-start = (f32[1,64,128]{2,1,0:T(8,128)S(1)}, f32[1,64,128]{2,1,0:T(8,128)S(1)}, u32[]{:S(2)}, u32[]{:S(2)}) collective-permute-start(f32[1,64,128]{2,1,0:T(8,128)S(1)} %get-tuple-element.37), channel_id=1, source_target_pairs={{0,1},{2,3},{4,5},{6,7},{8,9},{10,11},{12,13},{14,15},{16,17},{18,... | collective-permute-start | bytes 98312 | tf_op jit(solution)/shard_map/ppermute | solution.py:315
  12.6 5.8 %collective-permute-start.1 = (f32[1,64,128]{2,1,0:T(8,128)S(1)}, f32[1,64,128]{2,1,0:T(8,128)S(1)}, u32[]{:S(2)}, u32[]{:S(2)}) collective-permute-start(f32[1,64,128]{2,1,0:T(8,128)S(1)} %get-tuple-element.38), channel_id=1, source_target_pairs={{1,0},{3,2},{5,4},{7,6},{9,8},{11,10},{13,12},{15,14},{17,16},{19,... | collective-permute-start | bytes 98312 | tf_op jit(solution)/shard_map/ppermute | solution.py:316
  19.2 274.1 %reduce-scatter.2.cloned.1.call-start = ((), (), s32[]{:S(2)}) async-start(), calls=%async_computation.2 | async-start | bytes 5570560 | tf_op jit(solution)/shard_map/reduce_scatter | solution.py:325
  294.0 5.7 %collective-permute-start.2 = (f32[1,64,128]{2,1,0:T(8,128)S(1)}, f32[1,64,128]{2,1,0:T(8,128)S(1)}, u32[]{:S(2)}, u32[]{:S(2)}) collective-permute-start(f32[1,64,128]{2,1,0:T(8,128)S(1)} %get-tuple-element.36), channel_id=1, source_target_pairs={{0,1},{2,3},{4,5},{6,7},{8,9},{10,11},{12,13},{14,15},{16,17},{18,... | collective-permute-start | bytes 98312 | tf_op jit(solution)/shard_map/ppermute | solution.py:327
  297.4 5.8 %collective-permute-start.3 = (f32[1,64,128]{2,1,0:T(8,128)S(1)}, f32[1,64,128]{2,1,0:T(8,128)S(1)}, u32[]{:S(2)}, u32[]{:S(2)}) collective-permute-start(f32[1,64,128]{2,1,0:T(8,128)S(1)} %get-tuple-element.35), channel_id=1, source_target_pairs={{1,0},{3,2},{5,4},{7,6},{9,8},{11,10},{13,12},{15,14},{17,16},{19,... | collective-permute-start | bytes 98312 | tf_op jit(solution)/shard_map/ppermute | solution.py:328
Sparse Core Ops, SparseCore 0:
  19.3 56.0 all-gather.1
  216.2 76.9 reduce-scatter.1

commit v2 on v0

v2 whole, which is shorter than its diff:
```python
import math

import jax
import jax.numpy as jnp
from jax import lax
from jax.experimental import pallas as pl
from jax.experimental.pallas import tpu as pltpu
from jax.sharding import PartitionSpec as P

EDGE = 128
A_PROP = 0.1
LOSS_SCALE = 0.03125
LANES = 128
SUB = 8
COS = (0.9999999993567104, -0.4999999690796125, 0.041666428711172335, -0.0013882473076505886, 2.4093931432702378e-05)
SIN = (0.9999999999413409, -0.1666666638472293, 0.008333311638477454, -0.00019835422091007726, 2.6912728384156356e-06)


def split(value):
    high = value.astype(jnp.bfloat16)
    return high, (value - high.astype(jnp.float32)).astype(jnp.bfloat16)


def split_table(value):
    high = lax.reduce_precision(value, 8, 7)
    return high.astype(jnp.bfloat16), (value - high).astype(jnp.bfloat16)


def tables(size):
    half = jnp.arange(size // 2, dtype=jnp.int32)

    def wave(exponents):
        angles = -2.0 * math.pi / size * (exponents % size).astype(jnp.float32)
        scale = 1.0 / math.sqrt(size)
        return jnp.cos(angles) * scale, jnp.sin(angles) * scale

    def left(real, imag):
        high, low = split_table(jnp.block([[real, -imag], [imag, real]]))
        return jnp.concatenate([high, high, low], 1)

    def right(real, imag):
        high, low = split_table(jnp.block([[real, imag], [-imag, real]]))
        return jnp.concatenate([high, high, low], 0)

    even = wave(2 * half[:, None] * half[None, :])
    odd = wave((2 * half[:, None] + 1) * half[None, :])
    odd_back = wave(half[:, None] * (2 * half[None, :] + 1))
    return left(*even), left(*odd), left(*odd_back), right(*even), right(*odd), right(*odd_back)


def parity(width):
    columns = lax.broadcasted_iota(jnp.int32, (width, width), 1)
    rows = lax.broadcasted_iota(jnp.int32, (width, width), 0)
    source = columns % (width // 2) * 2 + columns // (width // 2)
    return (rows == source).astype(jnp.float32).astype(jnp.bfloat16)


def exact_dot(value, selection):
    high = value.astype(jnp.bfloat16)
    rest = value - high.astype(jnp.float32)
    middle = rest.astype(jnp.bfloat16)
    low = (rest - middle.astype(jnp.float32)).astype(jnp.bfloat16)
    total = jnp.dot(high, selection, preferred_element_type=jnp.float32)
    total = total + jnp.dot(middle, selection, preferred_element_type=jnp.float32)
    return total + jnp.dot(low, selection, preferred_element_type=jnp.float32)


def deal_kernel(x_ref, o_ref):
    pair = 2 * LANES
    selection = parity(pair)
    for k in range(x_ref.shape[1] // pair):
        dealt = exact_dot(x_ref[:, k * pair:(k + 1) * pair], selection)
        for p in range(2):
            o_ref[p, k] = dealt[:, p * LANES:(p + 1) * LANES]


def deal(value):
    rows, width = value.shape
    return pl.pallas_call(
        deal_kernel,
        out_shape=jax.ShapeDtypeStruct((2, width // (2 * LANES), rows, LANES), jnp.float32),
        name="deal",
    )(value)


def weave_kernel(x_ref, left_ref, right_ref, o_ref):
    pair = 2 * LANES
    rows = lax.broadcasted_iota(jnp.int32, (pair, pair), 0)
    columns = lax.broadcasted_iota(jnp.int32, (pair, pair), 1)
    selection = (columns == rows % LANES * 2 + rows // LANES).astype(jnp.float32).astype(jnp.bfloat16)
    lane = lax.broadcasted_iota(jnp.int32, o_ref.shape[:1] + (LANES,), 1)
    blocks = o_ref.shape[1] // pair
    for k in range(blocks):
        parts = []
        for p in range(2):
            value = x_ref[p, k]
            if k == 0:
                value = value + jnp.where(lane < EDGE // 2, left_ref[p], 0.0)
            if k == blocks - 1:
                value = value + jnp.where(lane >= LANES - EDGE // 2, right_ref[p], 0.0)
            parts.append(value)
        o_ref[:, k * pair:(k + 1) * pair] = exact_dot(jnp.concatenate(parts, 1), selection)


def weave(value, from_left, from_right):
    _, blocks, rows, _ = value.shape
    return pl.pallas_call(
        weave_kernel,
        out_shape=jax.ShapeDtypeStruct((rows, (blocks - 1) * 2 * LANES), jnp.float32),
        name="weave",
    )(value, from_left, from_right)


def kernel(
    rows_ref, columns_ref, count_ref,
    pieces_ref, probe_ref, low_ref, high_ref,
    left_even, left_odd, left_odd_back, right_even, right_odd, right_odd_back,
    out_ref,
    whole, total, base, ping, pong, first, second, turn, stack_even, stack_odd, wide_even, wide_odd, sems,
    *, blocks, slices,
):
    slot = pl.program_id(0)
    size = low_ref.shape[0]
    half = size // 2
    groups = size // SUB
    peers = pieces_ref.shape[0]
    height = pieces_ref.shape[2]
    lane = lax.broadcasted_iota(jnp.int32, (SUB, LANES), 1)

    def rows_of(device):
        return pl.ds(device * height, height)

    @pl.when(slot == 0)
    def _():
        copies = [
            pltpu.make_async_copy(pieces_ref.at[d], whole.at[:, rows_of(d), :], sems.at[0]) for d in range(peers)
        ]
        for copy in copies:
            copy.start()

        def clear(i, carry):
            for k in range(total.shape[0]):
                total[k, pl.ds(pl.multiple_of(i * SUB, SUB), SUB), :] = jnp.zeros((SUB, LANES), jnp.float32)
            return carry
        lax.fori_loop(0, total.shape[1] // SUB, clear, 0)
        for field in (base, ping, pong):
            for part in range(2):
                for p in range(2):
                    field[part, p, :SUB] = jnp.zeros((SUB, LANES), jnp.float32)
                    field[part, p, SUB + size:] = jnp.zeros((SUB, LANES), jnp.float32)
        for copy in copies:
            copy.wait()

    @pl.when(slot < count_ref[0])
    def _():
        start_row = rows_ref[slot]
        start_column = columns_ref[slot]
        sources = []
        for p in range(2):
            column = start_column + p
            at = (column + blocks * 2 * LANES) // 2
            side = lax.rem(column + blocks * 2 * LANES, 2)
            block = lax.rem(at // LANES, blocks)
            after = lax.rem(at // LANES + 1, blocks)
            sources.append((side * blocks + block, side * blocks + after, at % LANES))

        def tile(t):
            return slice(SUB + t * SUB, 2 * SUB + t * SUB)

        def window(t, j):
            rows = pl.ds(start_row + t * SUB, SUB)
            out = []
            for block, after, shift in sources:
                back = lax.rem(LANES - shift, LANES)
                here = pltpu.roll(whole[block * slices + j, rows, :], back, 1)
                there = pltpu.roll(whole[after * slices + j, rows, :], back, 1)
                out.append(jnp.where(lane < LANES - shift, here, there))
            return out

        def phase(t, j):
            out = []
            for value in window(t, j):
                theta = value - 1.0
                z = theta * theta
                c = COS[4]
                s = SIN[4]
                for k in (3, 2, 1, 0):
                    c = c * z + COS[k]
                    s = s * z + SIN[k]
                out.append((c, s * theta))
            return out

        def laplace(ref, part, t):
            even, odd = (ref[part, p, tile(t)] for p in range(2))
            row = SUB + t * SUB
            even_rows = ref[part, 0, row - 1:row + SUB - 1] + ref[part, 0, row + 1:row + SUB + 1]
            odd_rows = ref[part, 1, row - 1:row + SUB - 1] + ref[part, 1, row + 1:row + SUB + 1]
            even_columns = odd + jnp.where(lane == 0, 0.0, pltpu.roll(odd, 1, 1))
            odd_columns = even + jnp.where(lane == LANES - 1, 0.0, pltpu.roll(even, LANES - 1, 1))
            return (even_rows + even_columns) - 4.0 * even, (odd_rows + odd_columns) - 4.0 * odd

        def step(src, dst, factor):
            for t in range(groups):
                lap_re = laplace(src, 0, t)
                lap_im = laplace(src, 1, t)
                for p in range(2):
                    dst[0, p, tile(t)] = base[0, p, tile(t)] - factor * lap_im[p]
                    dst[1, p, tile(t)] = base[1, p, tile(t)] + factor * lap_re[p]

        def propagate():
            step(base, ping, A_PROP / 4)
            step(ping, pong, A_PROP / 3)
            step(pong, ping, A_PROP / 2)
            step(ping, pong, A_PROP)

        def enter(t, j, source, offset, kept):
            for p, (c, s) in enumerate(phase(t, j)):
                re = source[0, p, pl.ds(offset + t * SUB, SUB)]
                im = source[1, p, pl.ds(offset + t * SUB, SUB)]
                new_re, new_im = re * c - im * s, re * s + im * c
                base[0, p, tile(t)] = new_re
                base[1, p, tile(t)] = new_im
                kept[0, p, tile(t)] = new_re
                kept[1, p, tile(t)] = new_im
                if j == slices - 1:
                    turn[0, p, tile(t)] = c
                    turn[1, p, tile(t)] = s

        def leave(t, j, kept):
            rows = pl.ds(start_row + t * SUB, SUB)
            for p, (block, after, shift) in enumerate(sources):
                re = pong[0, p, tile(t)]
                im = pong[1, p, tile(t)]
                grad = -(re * kept[1, p, tile(t)] + im * kept[0, p, tile(t)])
                if j:
                    c = turn[0, p, tile(t)]
                    s = turn[1, p, tile(t)]
                    base[0, p, tile(t)] = re * c - im * s
                    base[1, p, tile(t)] = re * s + im * c
                rolled = pltpu.roll(grad, shift, 1)
                here = block * slices + j
                there = after * slices + j
                total[here, rows, :] = total[here, rows, :] + jnp.where(lane < shift, 0.0, rolled)
                total[there, rows, :] = total[there, rows, :] + jnp.where(lane < shift, rolled, 0.0)

        def dot(a, b):
            return jnp.dot(a[...], b[...], preferred_element_type=jnp.float32)

        def put_stack(stack, part, p, value):
            high, low = split(value)
            for k, piece in enumerate((high, low, high)):
                stack[k * size + part * half:k * size + (part + 1) * half, p * LANES:(p + 1) * LANES] = piece

        def put_wide(wide, rows, part, value):
            high, low = split(value)
            for k, piece in enumerate((high, low, high)):
                wide[rows, k * size + part * half:k * size + (part + 1) * half] = piece

        def lanes(k):
            return slice(k * LANES, (k + 1) * LANES)

        for t in range(groups):
            enter(t, 0, probe_ref, 0, first)
        propagate()
        for t in range(groups):
            enter(t, 1, pong, SUB, second)
        propagate()

        upper, lower = slice(0, half), slice(half, size)
        for part in range(2):
            for p in range(2):
                top = pong[part, p, SUB:SUB + half]
                bottom = pong[part, p, SUB + half:SUB + size]
                put_stack(stack_even, part, p, top + bottom)
                put_stack(stack_odd, part, p, top - bottom)
        for rows, inner in ((upper, dot(left_even, stack_even)), (lower, dot(left_odd, stack_odd))):
            for part, own in enumerate((upper, lower)):
                put_wide(wide_even, rows, part, inner[own, lanes(0)])
                put_wide(wide_odd, rows, part, inner[own, lanes(1)])
        even = dot(wide_even, right_even)
        odd = dot(wide_odd, right_odd)
        for k, rows in enumerate((upper, lower)):
            pulled = []
            for sign, data in ((1, low_ref), (-1, high_ref)):
                far_re = even[rows, lanes(0)] + sign * odd[rows, lanes(0)]
                far_im = even[rows, lanes(1)] + sign * odd[rows, lanes(1)]
                excess = (far_re * far_re + far_im * far_im) - data[pl.ds(k, half, stride=2), :]
                scaled = (4.0 * LOSS_SCALE) * excess
                pulled.append((scaled * far_re, -(scaled * far_im)))
            for part in range(2):
                put_wide(wide_even, rows, part, pulled[0][part] + pulled[1][part])
                put_wide(wide_odd, rows, part, pulled[0][part] - pulled[1][part])
        for p, inner in enumerate((dot(wide_even, right_even), dot(wide_odd, right_odd_back))):
            for part in range(2):
                put_stack(stack_even, part, p, inner[upper, lanes(part)])
                put_stack(stack_odd, part, p, inner[lower, lanes(part)])
        even = dot(left_even, stack_even)
        odd = dot(left_odd_back, stack_odd)
        for part, own in enumerate((upper, lower)):
            for p in range(2):
                base[part, p, SUB:SUB + half] = even[own, lanes(p)] + odd[own, lanes(p)]
                base[part, p, SUB + half:SUB + size] = even[own, lanes(p)] - odd[own, lanes(p)]

        propagate()
        for t in range(groups):
            leave(t, 1, second)
        propagate()
        for t in range(groups):
            leave(t, 0, first)

    @pl.when(slot == pl.num_programs(0) - 1)
    def _():
        copies = [
            pltpu.make_async_copy(total.at[:, rows_of(d), :], out_ref.at[d], sems.at[0]) for d in range(peers)
        ]
        for copy in copies:
            copy.start()
        for copy in copies:
            copy.wait()


def window_gradients(rows, columns, count, pieces, probe, measured, slices):
    slots, size = measured.shape[:2]
    peers, planes, height, _ = pieces.shape
    blocks = planes // (2 * slices)
    factors = tables(size)
    full = lambda a: pl.BlockSpec(a.shape, lambda k, *_: (0,) * a.ndim)
    field = pltpu.VMEM((2, 2, size + 2 * SUB, LANES), jnp.float32)
    plane = pltpu.VMEM((planes, peers * height, LANES), jnp.float32)
    tall = pltpu.VMEM((3 * size, size), jnp.bfloat16)
    wide = pltpu.VMEM((size, 3 * size), jnp.bfloat16)
    return pl.pallas_call(
        lambda *refs: kernel(*refs, blocks=blocks, slices=slices),
        grid_spec=pltpu.PrefetchScalarGridSpec(
            num_scalar_prefetch=3,
            grid=(slots,),
            in_specs=[
                pl.BlockSpec(memory_space=pl.ANY), full(probe),
                pl.BlockSpec((None, size, LANES), lambda k, *_: (k, 0, 0)),
                pl.BlockSpec((None, size, LANES), lambda k, *_: (k, 0, 1)),
                *[full(f) for f in factors],
            ],
            out_specs=pl.BlockSpec(memory_space=pl.ANY),
            scratch_shapes=[plane, plane] + [field] * 6 + [tall, tall, wide, wide, pltpu.SemaphoreType.DMA((1,))],
        ),
        out_shape=jax.ShapeDtypeStruct(pieces.shape, jnp.float32),
        compiler_params=pltpu.CompilerParams(vmem_limit_bytes=48 * 2**20),
        name="windows",
    )(rows, columns, count, pieces, probe, measured, measured, *factors)


def shards(potential, probe_wave, offsets, members, counts, measured):
    slices, height, own_width = potential.shape
    size = probe_wave.shape[-1]
    strips = lax.axis_size("strip")
    up = [(i, i + 1) for i in range(strips - 1)]
    down = [(j, i) for i, j in up]
    own = deal(potential.reshape(slices * height, own_width))
    from_left = lax.ppermute(own[:, -1], "strip", up)
    from_right = lax.ppermute(own[:, 0], "strip", down)
    lane = lax.broadcasted_iota(jnp.int32, from_left.shape, 2)
    edges = jnp.where(lane < EDGE // 2, from_right, from_left)
    piece = jnp.concatenate([own, edges[:, None]], 1)
    blocks = piece.shape[1]
    gathered = lax.all_gather(piece.reshape(-1, LANES), "probe", axis=0, tiled=False)
    positions = members[0, 0]
    rows = offsets[0, 0][positions]
    columns = offsets[0, 1][positions]
    probe = deal(probe_wave.reshape(2 * size, size)).reshape(2, 2, size, LANES).transpose(1, 0, 2, 3)
    gradient = window_gradients(
        rows, columns, counts[0], gathered.reshape(-1, 2 * blocks * slices, height, LANES), probe, measured[0, 0], slices
    )
    mine = lax.psum_scatter(gradient.reshape(gathered.shape), "probe", scatter_dimension=0, tiled=False)
    mine = mine.reshape(2, blocks, slices * height, LANES)
    from_left = lax.ppermute(mine[:, -1], "strip", up)
    from_right = lax.ppermute(mine[:, -1], "strip", down)
    return weave(mine, from_left, from_right).reshape(potential.shape)


def solution(mesh):
    placed = (
        P(None, "probe", "strip"),
        P(),
        P("strip", None, None),
        P("strip", "probe", None),
        P("strip", "probe"),
        P("strip", "probe", None, None, None),
    )
    return jax.shard_map(
        shards, mesh=mesh, in_specs=placed, out_specs=P(None, "probe", "strip"), check_vma=False
    )
```

time: 487 us -> 220 us (0.45)
  starting transfers between devices: 216 us -> 12 us
  matrix products: 47.6 us -> 0 us
  local copies, waits for them, and re-layouts: 40.2 us -> 8.46 us
  Pallas kernels: 0 us -> 30.7 us
  other arithmetic: 19.1 us -> 5.27 us
  waiting for transfers between devices: 135 us -> 148 us
  loops' own time: 12.7 us -> 0 us
    ppermute x4, starting transfers between devices: 216 us -> 12 us  [the longest x1 4.87 us: shards(): from_left = lax.ppermute(own[:, -1], 'strip', up)]
    dot_general x32 -> x0, matrix products: 47.6 us -> none  [matmul(): jnp.dot(left_side, right_side, precision=lax.Precision.HIGHEST, preferred...]
    pallas_call x0 -> x4, Pallas kernels: none -> 30.7 us  [the longest x1 24.3 us: window_gradients(): pl.pallas_call(lambda *refs: kernel(*refs, blocks=blocks, slices=slices),...]
    reduce_scatter x1, waiting for transfers between devices: 72.8 us -> 94.8 us  [shards(): lax.psum_scatter(gradient.reshape(gathered.shape), 'probe', scatter_dimen...]
    dynamic_update_slice x4 -> x0, local copies, waits for them, and re-layouts: 13.2 us -> none  [visit(): lax.dynamic_update_slice(gradient, current + window_grad, (anchor, start_...]
    another operation x1 -> x0, loops' own time: 12.7 us -> none  [shards(): lax.fori_loop(0, counts[0, 0], visit, jnp.zeros(whole_object.shape, jnp.f...]
    slice x5 -> x0, local copies, waits for them, and re-layouts: 12 us -> none  [the longest x2 5.18 us: exit_wave(): phases = window[slice_index]]
    mul x40 -> x1, other arithmetic: 9.92 us -> 0.01 us  [tables(): even = wave(2 * half[:, None] * half[None, :])]
  transfers between devices with their start and end apart: 6 -> 6, of which waited for: 6 -> 6; matrix products, arithmetic and copies ran while one was open for 2% -> 3% of each run, Pallas kernels for 0% -> 1%
where the time goes in v2:
time: 220 us; the launch traced here: 219 us
  waiting for transfers between devices  148 us (67%)
  Pallas kernels  30.7 us (14%)
  between operations  14.3 us (6%)
  starting transfers between devices  12 us (5%)
  local copies, waits for them, and re-layouts  8.46 us (4%)
  other arithmetic  5.27 us (2%)
    reduce_scatter x1, waiting for transfers between devices, shards(): lax.psum_scatter(gradient.reshape(gathered.shape), 'probe', scatter_dimen...  94.8 us
    all_gather x1, waiting for transfers between devices, shards(): lax.all_gather(piece.reshape(-1, LANES), 'probe', axis=0, tiled=False)  46.4 us
    pallas_call x1, Pallas kernels, window_gradients(): pl.pallas_call(lambda *refs: kernel(*refs, blocks=blocks, slices=slices),...  24.3 us
    ppermute x1, starting transfers between devices, shards(): from_left = lax.ppermute(own[:, -1], 'strip', up)  4.87 us
    ppermute x1, starting transfers between devices, shards(): from_left = lax.ppermute(mine[:, -1], 'strip', up)  4.55 us
  transfers between devices with their start and end apart: 6, of which 6 were waited for; matrix products, arithmetic and copies ran while one was open for 3% of the time, Pallas kernels for 1%

profile of v2, /device:TPU:0, one launch (start us, length us, event | category | flops | bytes accessed | tf_op | source)
XLA Modules:
  0.0 218.7 jit_solution(1131666034050342364)
XLA Ops:
  6.5 2.0 deal.2
  8.6 0.9 slice_bitcast_fusion.1
  9.5 4.9 %collective-permute-start.1 = (f32[2,64,128]{2,1,0:T(8,128)S(1)}, f32[2,64,128]{2,1,0:T(8,128)S(1)}, u32[]{:S(2)}, u32[]{:S(2)}) collective-permute-start(f32[2,64,128]{2,1,0:T(8,128)S(1)} %get-tuple-element.5), channel_id=1, source_target_pairs={{0,1},{2,3},{4,5},{6,7},{8,9},{10,11},{12,13},{14,15},{16,17},{18,... | collective-permute-start | bytes 196616 | tf_op jit(solution)/shard_map/ppermute | solution.py:359
  14.4 1.3 collective-permute-start
  16.2 4.3 %collective-permute-done = f32[2,64,128]{2,1,0:T(8,128)S(1)} collective-permute-done((f32[2,64,128]{2,1,0:T(8,128)S(1)}, f32[2,64,128]{2,1,0:T(8,128)S(1)}, u32[]{:S(2)}, u32[]{:S(2)}) %collective-permute-start) | collective-permute-done | bytes 65568 | tf_op jit(solution)/shard_map/ppermute | solution.py:360
  20.5 1.7 pad_maximum_fusion.18
  23.1 0.7 fusion.33
  23.7 0.8 slice_bitcast_fusion.3
  25.1 0.6 gather_fusion
  25.8 2.2 %deal.3 = f32[2,1,512,128]{3,2,1,0:T(8,128)} custom-call(f32[512,256]{1,0:T(8,128)} %bitcast.43), custom_call_target="tpu_custom_call" | custom-call | tf_op jit(solution)/shard_map/deal/pallas_call | solution.py:79
  28.0 1.1 copy.22
  30.3 0.8 pad_maximum_fusion.3
  31.1 0.9 pad_maximum_fusion
  32.0 46.4 %all-gather.2.cloned.1.call-done = f32[16,640,128]{2,1,0:T(8,128)} async-done(((f32[1,640,128]{2,1,0:T(8,128)}), f32[16,640,128]{2,1,0:T(8,128)}) %all-gather.2.cloned.1.call-update) | async-done | bytes 5242896 | tf_op jit(solution)/shard_map/all_gather | solution.py:365
  78.5 1.0 copy-done.1
  79.5 1.0 copy-done.2
  80.5 1.0 copy-done.3
  81.5 24.3 %windows.1 = f32[16,20,32,128]{3,2,1,0:T(8,128)} custom-call(s32[6]{0:T(128)S(1)} %gather_fusion, s32[6]{0:T(128)S(1)} %gather_fusion.1, s32[1]{0:T(128)} %bitcast.35.refs_2_, f32[16,20,32,128]{3,2,1,0:T(8,128)} %bitcast.40, f32[2,2,256,128]{3,2,1,0:T(8,128)S(1)} %bitcast.38, f32[6,256,256]{2,1,0:T(8,128)S(1)} %bitcast.36, f32[6,256,256]{2,1,0:T(8,128)S(1)} %bitcast.37, ...), custom_call_target="tpu_custom_call" | custom-call | tf_op jit(solution)/shard_map/windows/pallas_call | solution.py:332
  105.8 94.8 %reduce-scatter.2.cloned.1.call-done = f32[1,640,128]{2,1,0:T(8,128)} async-done(((f32[16,640,128]{2,1,0:T(8,128)}), f32[1,640,128]{2,1,0:T(8,128)}) %reduce-scatter.2.cloned.1.call-update) | async-done | bytes 327696 | tf_op jit(solution)/shard_map/reduce_scatter | solution.py:373
  200.6 0.8 slice_bitcast_fusion
  201.4 1.3 collective-permute-start.3
  202.7 4.5 %collective-permute-start.2 = (f32[2,64,128]{2,1,0:T(8,128)S(1)}, f32[2,64,128]{2,1,0:T(8,128)S(1)}, u32[]{:S(2)}, u32[]{:S(2)}) collective-permute-start(f32[2,64,128]{2,1,0:T(8,128)S(1)} %slice_bitcast_fusion), channel_id=1, source_target_pairs={{0,1},{2,3},{4,5},{6,7},{8,9},{10,11},{12,13},{14,15},{16,17},{18,... | collective-permute-start | bytes 196616 | tf_op jit(solution)/shard_map/ppermute | solution.py:375
  207.6 1.6 collective-permute-done.2.left_ref
  209.8 2.1 weave.1
  (28 shorter events, 3.4 us)
Async XLA Ops:
  6.5 71.9 %all-gather.2.cloned.1.call-start = ((), (), s32[]{:S(2)}) async-start(), calls=%async_computation.1 | async-start | bytes 5570560 | tf_op jit(solution)/shard_map/all_gather | solution.py:365
  9.5 6.8 %collective-permute-start.1 = (f32[2,64,128]{2,1,0:T(8,128)S(1)}, f32[2,64,128]{2,1,0:T(8,128)S(1)}, u32[]{:S(2)}, u32[]{:S(2)}) collective-permute-start(f32[2,64,128]{2,1,0:T(8,128)S(1)} %get-tuple-element.5), channel_id=1, source_target_pairs={{0,1},{2,3},{4,5},{6,7},{8,9},{10,11},{12,13},{14,15},{16,17},{18,... | collective-permute-start | bytes 196616 | tf_op jit(solution)/shard_map/ppermute | solution.py:359
  14.4 6.2 %collective-permute-start = (f32[2,64,128]{2,1,0:T(8,128)S(1)}, f32[2,64,128]{2,1,0:T(8,128)S(1)}, u32[]{:S(2)}, u32[]{:S(2)}) collective-permute-start(f32[2,64,128]{2,1,0:T(8,128)S(1)} %get-tuple-element.6), channel_id=1, source_target_pairs={{1,0},{3,2},{5,4},{7,6},{9,8},{11,10},{13,12},{15,14},{17,16},{19,... | collective-permute-start | bytes 196616 | tf_op jit(solution)/shard_map/ppermute | solution.py:360
  22.2 56.2 %copy-start = (f32[1,1,6,256,256]{4,3,2,1,0:T(8,128)S(1)}, f32[1,1,6,256,256]{4,3,2,1,0:T(8,128)}, u32[]{:S(2)}) copy-start(f32[1,1,6,256,256]{4,3,2,1,0:T(8,128)} %param.11) | copy-start | bytes 4718596
  22.3 178.3 %reduce-scatter.2.cloned.1.call-start = ((), (), s32[]{:S(2)}) async-start(), calls=%async_computation.2 | async-start | bytes 5570560 | tf_op jit(solution)/shard_map/reduce_scatter | solution.py:373
  78.5 1.0 copy-start.1
  79.5 1.0 copy-start.2
  80.5 1.0 copy-start.3
  201.4 6.1 %collective-permute-start.3 = (f32[2,64,128]{2,1,0:T(8,128)S(1)}, f32[2,64,128]{2,1,0:T(8,128)S(1)}, u32[]{:S(2)}, u32[]{:S(2)}) collective-permute-start(f32[2,64,128]{2,1,0:T(8,128)S(1)} %slice_bitcast_fusion), channel_id=1, source_target_pairs={{1,0},{3,2},{5,4},{7,6},{9,8},{11,10},{13,12},{15,14},{17,16},{19,... | collective-permute-start | bytes 196616 | tf_op jit(solution)/shard_map/ppermute | solution.py:376
  202.7 6.4 %collective-permute-start.2 = (f32[2,64,128]{2,1,0:T(8,128)S(1)}, f32[2,64,128]{2,1,0:T(8,128)S(1)}, u32[]{:S(2)}, u32[]{:S(2)}) collective-permute-start(f32[2,64,128]{2,1,0:T(8,128)S(1)} %slice_bitcast_fusion), channel_id=1, source_target_pairs={{0,1},{2,3},{4,5},{6,7},{8,9},{10,11},{12,13},{14,15},{16,17},{18,... | collective-permute-start | bytes 196616 | tf_op jit(solution)/shard_map/ppermute | solution.py:375
  207.6 1.6 copy-start.4
  209.2 0.6 copy-start.5
Sparse Core Ops, SparseCore 0:
  22.4 56.0 all-gather.1
  105.9 94.6 reduce-scatter.1

commit v3 on v2

--- a/solution.py
+++ b/solution.py
@@ -1,3 +1,4 @@
+import functools
 import math
 
 import jax
@@ -26,8 +27,8 @@
     return high.astype(jnp.bfloat16), (value - high).astype(jnp.bfloat16)
 
 
-def tables(size):
-    half = jnp.arange(size // 2, dtype=jnp.int32)
+def tables(size, zero):
+    half = jnp.arange(size // 2, dtype=jnp.int32) + zero
 
     def wave(exponents):
         angles = -2.0 * math.pi / size * (exponents % size).astype(jnp.float32)
@@ -65,25 +66,34 @@
     return total + jnp.dot(low, selection, preferred_element_type=jnp.float32)
 
 
-def deal_kernel(x_ref, o_ref):
+def deal_kernel(*refs):
+    *sources, o_ref = refs
     pair = 2 * LANES
     selection = parity(pair)
-    for k in range(x_ref.shape[1] // pair):
-        dealt = exact_dot(x_ref[:, k * pair:(k + 1) * pair], selection)
+    at = 0
+    for block in range(o_ref.shape[1]):
+        if at < sources[0].shape[1]:
+            value = sources[0][:, at:at + pair]
+        else:
+            value = jnp.concatenate([ref[...] for ref in sources[1:]], 1)
+        at += pair
+        dealt = exact_dot(value, selection)
         for p in range(2):
-            o_ref[p, k] = dealt[:, p * LANES:(p + 1) * LANES]
-
-
-def deal(value):
+            o_ref[p, block] = dealt[:, p * LANES:(p + 1) * LANES]
+
+
+def deal(value, *edges):
     rows, width = value.shape
+    blocks = (width + sum(e.shape[1] for e in edges)) // (2 * LANES)
     return pl.pallas_call(
         deal_kernel,
-        out_shape=jax.ShapeDtypeStruct((2, width // (2 * LANES), rows, LANES), jnp.float32),
+        out_shape=jax.ShapeDtypeStruct((2, blocks, rows, LANES), jnp.float32),
         name="deal",
-    )(value)
-
-
-def weave_kernel(x_ref, left_ref, right_ref, o_ref):
+    )(value, *edges)
+
+
+def weave_kernel(*refs):
+    *terms, left_ref, right_ref, o_ref = refs
     pair = 2 * LANES
     rows = lax.broadcasted_iota(jnp.int32, (pair, pair), 0)
     columns = lax.broadcasted_iota(jnp.int32, (pair, pair), 1)
@@ -93,7 +103,9 @@
     for k in range(blocks):
         parts = []
         for p in range(2):
-            value = x_ref[p, k]
+            value = terms[0][p, k]
+            for term in terms[1:]:
+                value = value + term[p, k]
             if k == 0:
                 value = value + jnp.where(lane < EDGE // 2, left_ref[p], 0.0)
             if k == blocks - 1:
@@ -102,38 +114,42 @@
         o_ref[:, k * pair:(k + 1) * pair] = exact_dot(jnp.concatenate(parts, 1), selection)
 
 
-def weave(value, from_left, from_right):
-    _, blocks, rows, _ = value.shape
+def weave(terms, from_left, from_right):
+    _, blocks, rows, _ = terms[0].shape
     return pl.pallas_call(
         weave_kernel,
         out_shape=jax.ShapeDtypeStruct((rows, (blocks - 1) * 2 * LANES), jnp.float32),
         name="weave",
-    )(value, from_left, from_right)
+    )(*terms, from_left, from_right)
 
 
 def kernel(
     rows_ref, columns_ref, count_ref,
-    pieces_ref, probe_ref, low_ref, high_ref,
+    place_ref, probe_ref, low_ref, high_ref,
     left_even, left_odd, left_odd_back, right_even, right_odd, right_odd_back,
-    out_ref,
+    pieces, outs,
     whole, total, base, ping, pong, first, second, turn, stack_even, stack_odd, wide_even, wide_odd, sems,
-    *, blocks, slices,
+    *, blocks, slices, grid,
 ):
     slot = pl.program_id(0)
     size = low_ref.shape[0]
     half = size // 2
     groups = size // SUB
-    peers = pieces_ref.shape[0]
-    height = pieces_ref.shape[2]
+    height = pieces[0].shape[1]
+    offsets = [(a, b, c) for a in range(grid[0]) for b in range(grid[1]) for c in range(grid[2])]
     lane = lax.broadcasted_iota(jnp.int32, (SUB, LANES), 1)
 
-    def rows_of(device):
-        return pl.ds(device * height, height)
+    def rows_of(offset, sign):
+        device = 0
+        for axis, count in enumerate(grid):
+            device = device * count + lax.rem(place_ref[axis] + sign * offset[axis] + count, count)
+        return pl.ds(pl.multiple_of(device * height, height), height)
 
     @pl.when(slot == 0)
     def _():
         copies = [
-            pltpu.make_async_copy(pieces_ref.at[d], whole.at[:, rows_of(d), :], sems.at[0]) for d in range(peers)
+            pltpu.make_async_copy(piece, whole.at[:, rows_of(offset, -1), :], sems.at[0])
+            for piece, offset in zip(pieces, offsets)
         ]
         for copy in copies:
             copy.start()
@@ -311,7 +327,8 @@
     @pl.when(slot == pl.num_programs(0) - 1)
     def _():
         copies = [
-            pltpu.make_async_copy(total.at[:, rows_of(d), :], out_ref.at[d], sems.at[0]) for d in range(peers)
+            pltpu.make_async_copy(total.at[:, rows_of(offset, 1), :], outs[offset[0] * grid[2] + offset[2]].at[offset[1]], sems.at[0])
+            for offset in offsets
         ]
         for copy in copies:
             copy.start()
@@ -319,61 +336,169 @@
             copy.wait()
 
 
-def window_gradients(rows, columns, count, pieces, probe, measured, slices):
+def window_gradients(rows, columns, count, place, pieces, grid, probe, measured, slices, zero):
     slots, size = measured.shape[:2]
-    peers, planes, height, _ = pieces.shape
+    planes, height, _ = pieces[0].shape
+    peers = len(pieces)
     blocks = planes // (2 * slices)
-    factors = tables(size)
+    factors = tables(size, zero)
     full = lambda a: pl.BlockSpec(a.shape, lambda k, *_: (0,) * a.ndim)
+    anywhere = pl.BlockSpec(memory_space=pl.ANY)
     field = pltpu.VMEM((2, 2, size + 2 * SUB, LANES), jnp.float32)
     plane = pltpu.VMEM((planes, peers * height, LANES), jnp.float32)
     tall = pltpu.VMEM((3 * size, size), jnp.bfloat16)
     wide = pltpu.VMEM((size, 3 * size), jnp.bfloat16)
+    groups = grid[0] * grid[2]
+
+    def body(*refs):
+        scalars, refs = refs[:4], refs[4:]
+        fixed, refs = refs[:9], refs[9:]
+        return kernel(
+            *scalars, *fixed, refs[:peers], refs[peers:peers + groups], *refs[peers + groups:],
+            blocks=blocks, slices=slices, grid=grid,
+        )
+
     return pl.pallas_call(
-        lambda *refs: kernel(*refs, blocks=blocks, slices=slices),
+        body,
         grid_spec=pltpu.PrefetchScalarGridSpec(
-            num_scalar_prefetch=3,
+            num_scalar_prefetch=4,
             grid=(slots,),
             in_specs=[
-                pl.BlockSpec(memory_space=pl.ANY), full(probe),
+                full(probe),
                 pl.BlockSpec((None, size, LANES), lambda k, *_: (k, 0, 0)),
                 pl.BlockSpec((None, size, LANES), lambda k, *_: (k, 0, 1)),
                 *[full(f) for f in factors],
+                *[anywhere for _ in pieces],
             ],
-            out_specs=pl.BlockSpec(memory_space=pl.ANY),
+            out_specs=[anywhere] * groups,
             scratch_shapes=[plane, plane] + [field] * 6 + [tall, tall, wide, wide, pltpu.SemaphoreType.DMA((1,))],
         ),
-        out_shape=jax.ShapeDtypeStruct(pieces.shape, jnp.float32),
+        out_shape=[jax.ShapeDtypeStruct((grid[1], planes, height, LANES), jnp.float32)] * groups,
         compiler_params=pltpu.CompilerParams(vmem_limit_bytes=48 * 2**20),
         name="windows",
-    )(rows, columns, count, pieces, probe, measured, measured, *factors)
-
-
-def shards(potential, probe_wave, offsets, members, counts, measured):
+    )(rows, columns, count, place, probe, measured, measured, *factors, *pieces)
+
+
+def grid_of(devices):
+    count = len(devices)
+    cores = len({d.core_on_chip for d in devices})
+    chips = [tuple(devices[i].coords) for i in range(0, count, cores)]
+    fast = 1
+    if len(chips) > 1:
+        moving = [a != b for a, b in zip(chips[0], chips[1])]
+        while fast < len(chips) and all(m or a == b for m, a, b in zip(moving, chips[0], chips[fast])):
+            fast += 1
+    if len(chips) % fast:
+        fast = 1
+    return len(chips) // fast, fast, cores
+
+
+def shards(potential, probe_wave, offsets, members, counts, measured, *, grid):
     slices, height, own_width = potential.shape
     size = probe_wave.shape[-1]
     strips = lax.axis_size("strip")
     up = [(i, i + 1) for i in range(strips - 1)]
     down = [(j, i) for i, j in up]
-    own = deal(potential.reshape(slices * height, own_width))
-    from_left = lax.ppermute(own[:, -1], "strip", up)
-    from_right = lax.ppermute(own[:, 0], "strip", down)
-    lane = lax.broadcasted_iota(jnp.int32, from_left.shape, 2)
-    edges = jnp.where(lane < EDGE // 2, from_right, from_left)
-    piece = jnp.concatenate([own, edges[:, None]], 1)
+    slow, fast, cores = grid
+
+    def moved(value, a, b, c):
+        if not (a or b or c):
+            return value
+        pairs = []
+        for z in range(slow):
+            for y in range(fast):
+                for core in range(cores):
+                    to = ((z + a) % slow * fast + (y + b) % fast) * cores + (core + c) % cores
+                    pairs.append(((z * fast + y) * cores + core, to))
+        return lax.ppermute(value, "probe", pairs)
+
+    def along(value, to, valid):
+        pairs = []
+        for z in range(slow):
+            if 0 <= z + to < slow and valid(z + to):
+                for rest in range(fast * cores):
+                    pairs.append((z * fast * cores + rest, (z + to) * fast * cores + rest))
+        return lax.ppermute(value, "probe", pairs)
+
+    def after(value, *done):
+        return lax.optimization_barrier((value, *done))[0]
+
+    flat = potential.reshape(slices * height, own_width)
+    from_left = lax.ppermute(flat[:, own_width - EDGE:], "strip", up)
+    from_right = lax.ppermute(flat[:, :EDGE], "strip", down)
+    piece = deal(flat, from_right, from_left)
+    piece, probe_wave, offsets, members, zero = lax.optimization_barrier(
+        (piece, probe_wave, offsets, members, jnp.zeros((), jnp.int32))
+    )
     blocks = piece.shape[1]
-    gathered = lax.all_gather(piece.reshape(-1, LANES), "probe", axis=0, tiled=False)
+    piece = piece.reshape(2 * blocks * slices, height, LANES)
+
+    lines = {0: piece}
+    if slow > 1:
+        lines[1] = moved(piece, 1, 0, 0)
+    if slow > 2:
+        lines[slow - 1] = moved(after(piece, lines[1]), slow - 1, 0, 0)
+        right, left = {1: lines[1]}, {1: lines[slow - 1]}
+        for k in range(2, slow - 1):
+            right[k] = along(right[k - 1], 1, lambda z: z >= k)
+            left[k] = along(left[k - 1], -1, lambda z: z <= slow - 1 - k)
+        for k in range(2, slow - 1):
+            lines[k] = right[k] + left[slow - k]
+    order = [0] + [k for k in (1, slow - 1) if 0 < k < slow] + list(range(2, slow - 1))
+    order = list(dict.fromkeys(order))
+    held = {}
+    previous = None
+    for a in order:
+        held[a, 0] = lines[a]
+        for b in range(1, fast):
+            source = lines[a] if previous is None else after(lines[a], previous)
+            previous = held[a, b] = moved(source, 0, b, 0)
+    pieces = []
+    for a in range(slow):
+        for b in range(fast):
+            for c in range(cores):
+                pieces.append(moved(held[a, b], 0, 0, c))
+
     positions = members[0, 0]
     rows = offsets[0, 0][positions]
     columns = offsets[0, 1][positions]
+    me = lax.axis_index("probe")
+    place = jnp.stack([me // (fast * cores), me // cores % fast, me % cores]).astype(jnp.int32)
     probe = deal(probe_wave.reshape(2 * size, size)).reshape(2, 2, size, LANES).transpose(1, 0, 2, 3)
-    gradient = window_gradients(
-        rows, columns, counts[0], gathered.reshape(-1, 2 * blocks * slices, height, LANES), probe, measured[0, 0], slices
-    )
-    mine = lax.psum_scatter(gradient.reshape(gathered.shape), "probe", scatter_dimension=0, tiled=False)
-    mine = mine.reshape(2, blocks, slices * height, LANES)
-    from_left = lax.ppermute(mine[:, -1], "strip", up)
-    from_right = lax.ppermute(mine[:, -1], "strip", down)
+    terms = window_gradients(rows, columns, counts[0], place, pieces, grid, probe, measured[0, 0], slices, zero)
+
+    chip = {}
+    for a in range(slow):
+        own = terms[a * cores]
+        for c in range(1, cores):
+            own = own + moved(terms[a * cores + c], 0, 0, c)
+        chip[a] = own
+    line = {}
+    previous = None
+    for a in reversed(order):
+        total = chip[a][0]
+        for b in range(1, fast):
+            source = chip[a][b] if previous is None else after(chip[a][b], previous)
+            previous = moved(source, 0, b, 0)
+            total = total + previous
+        line[a] = total
+    mine = [line[0]]
+    right, left = None, None
+    for k in range(slow - 2, 1, -1):
+        right = line[k] if right is None else line[k] + right
+        left = line[slow - k] if left is None else line[slow - k] + left
+        right = along(right, 1, lambda z: z <= slow - k)
+        left = along(left, -1, lambda z: z >= k - 1)
+    if slow > 1:
+        first = line[1] if right is None else line[1] + right
+        mine.append(moved(first, 1, 0, 0))
+    if slow > 2:
+        last = line[slow - 1] if left is None else line[slow - 1] + left
+        mine.append(moved(last, slow - 1, 0, 0))
+    mine = [term.reshape(2, blocks, slices * height, LANES) for term in mine]
+    edges = sum(term[:, -1] for term in mine[1:]) + mine[0][:, -1]
+    from_left = lax.ppermute(edges, "strip", up)
+    from_right = lax.ppermute(edges, "strip", down)
     return weave(mine, from_left, from_right).reshape(potential.shape)
 
 
@@ -386,6 +511,7 @@
         P("strip", "probe"),
         P("strip", "probe", None, None, None),
     )
+    grid = grid_of(list(mesh.devices[:, 0]))
     return jax.shard_map(
-        shards, mesh=mesh, in_specs=placed, out_specs=P(None, "probe", "strip"), check_vma=False
+        functools.partial(shards, grid=grid), mesh=mesh, in_specs=placed, out_specs=P(None, "probe", "strip"), check_vma=False
     )

time: 220 us -> 153 us (0.70)
  waiting for transfers between devices: 148 us -> 54.2 us
  starting transfers between devices: 12 us -> 57.3 us
  between operations: 14.3 us -> 1.1 us
  Pallas kernels: 30.7 us -> 26.7 us
  local copies, waits for them, and re-layouts: 8.46 us -> 6.07 us
    reduce_scatter x1 -> x0, waiting for transfers between devices: 94.8 us -> none  [shards(): lax.psum_scatter(gradient.reshape(gathered.shape), 'probe', scatter_dimen...]
    ppermute x4 -> x32, waiting for transfers between devices: 6.73 us -> 54.2 us  [the longest x24 41 us: moved(): return lax.ppermute(value, 'probe', pairs)]
    all_gather x1 -> x0, waiting for transfers between devices: 46.4 us -> none  [shards(): lax.all_gather(piece.reshape(-1, LANES), 'probe', axis=0, tiled=False)]
    ppermute x4 -> x32, starting transfers between devices: 12 us -> 57.3 us  [the longest x24 41.3 us: moved(): return lax.ppermute(value, 'probe', pairs)]
    pallas_call x3, Pallas kernels: 28.6 us -> 24.4 us  [the longest x1 20 us: window_gradients(): pl.pallas_call(body, grid_spec=pltpu.PrefetchScalarGridSpec(num_scalar_pr...]
    unnamed x12 -> x24, local copies, waits for them, and re-layouts: 3.62 us -> 1.27 us
  transfers between devices with their start and end apart: 6 -> 32, of which waited for: 6 -> 15; matrix products, arithmetic and copies ran while one was open for 3% -> 7% of each run, Pallas kernels for 1% -> 1%
where the time goes in v3:
time: 153 us; the launch traced here: 152 us
  starting transfers between devices  57.3 us (37%)
  waiting for transfers between devices  54.2 us (35%)
  Pallas kernels  26.7 us (17%)
  other arithmetic  6.76 us (4%)
  local copies, waits for them, and re-layouts  6.07 us (4%)
    ppermute x24, starting transfers between devices, moved(): return lax.ppermute(value, 'probe', pairs)  41.3 us
    ppermute x24, waiting for transfers between devices, moved(): return lax.ppermute(value, 'probe', pairs)  41 us
    pallas_call x1, Pallas kernels, window_gradients(): pl.pallas_call(body, grid_spec=pltpu.PrefetchScalarGridSpec(num_scalar_pr...  20 us
    ppermute x4, waiting for transfers between devices, along(): return lax.ppermute(value, 'probe', pairs)  7.62 us
    ppermute x1, starting transfers between devices, shards(): from_left = lax.ppermute(flat[:, own_width - EDGE:], 'strip', up)  4.86 us
    ppermute x1, starting transfers between devices, shards(): from_left = lax.ppermute(edges, 'strip', up)  4.55 us
    pallas_call x2, Pallas kernels, deal(): pl.pallas_call(deal_kernel, out_shape=jax.ShapeDtypeStruct((2, blocks, ro...  4.42 us
    ppermute x4, starting transfers between devices, along(): return lax.ppermute(value, 'probe', pairs)  3.95 us
  transfers between devices with their start and end apart: 32, of which 15 were waited for; matrix products, arithmetic and copies ran while one was open for 7% of the time, Pallas kernels for 1%

profile of v3, /device:TPU:0, one launch (start us, length us, event | category | flops | bytes accessed | tf_op | source)
XLA Modules:
  0.0 152.1 jit_solution(3309824978433445020)
XLA Ops:
  0.8 4.9 %collective-permute-start.1 = (f32[64,128]{1,0:T(8,128)S(1)}, f32[64,128]{1,0:T(8,128)S(1)}, u32[]{:S(2)}, u32[]{:S(2)}) collective-permute-start(f32[64,128]{1,0:T(8,128)S(1)} %get-tuple-element.45), channel_id=1, source_target_pairs={{0,1},{2,3},{4,5},{6,7},{8,9},{10,11},{12,13},{14,15},{16,17},{18,... | collective-permute-start | bytes 98312 | tf_op jit(solution)/shard_map/ppermute | solution.py:427
  7.7 3.7 %collective-permute-done.refs_1_ = f32[64,128]{1,0:T(8,128)S(1)} collective-permute-done((f32[64,128]{1,0:T(8,128)S(1)}, f32[64,128]{1,0:T(8,128)S(1)}, u32[]{:S(2)}, u32[]{:S(2)}) %collective-permute-start) | collective-permute-done | bytes 32800 | tf_op jit(solution)/shard_map/ppermute | solution.py:428
  12.1 2.2 %deal.2 = f32[2,5,64,128]{3,2,1,0:T(8,128)} custom-call(f32[64,1024]{1,0:T(8,128)} %bitcast.88, f32[64,128]{1,0:T(8,128)} %copy-done.10, f32[64,128]{1,0:T(8,128)} %copy-done.9), custom_call_target="tpu_custom_call" | custom-call | tf_op jit(solution)/shard_map/deal/pallas_call | solution.py:88
  14.3 1.6 %collective-permute-start.5 = (f32[20,32,128]{2,1,0:T(8,128)}, f32[20,32,128]{2,1,0:T(8,128)S(1)}, u32[]{:S(2)}, u32[]{:S(2)}) collective-permute-start(f32[20,32,128]{2,1,0:T(8,128)} %bitcast.71), channel_id=1, source_target_pairs={{0,8},{2,10},{4,12},{6,14},{8,16},{10,18},{12,20},{14,22},{16,24},... | collective-permute-start | bytes 983048 | tf_op jit(solution)/shard_map/ppermute | solution.py:413
  20.1 2.2 %deal.3 = f32[2,1,512,128]{3,2,1,0:T(8,128)} custom-call(f32[512,256]{1,0:T(8,128)} %bitcast.82), custom_call_target="tpu_custom_call" | custom-call | tf_op jit(solution)/shard_map/deal/pallas_call | solution.py:88
  22.3 1.9 %copy.18 = f32[2,2,256,128]{3,2,0,1:T(8,128)} copy(f32[2,2,256,128]{3,2,1,0:T(8,128)} %bitcast.79) | data formatting | bytes 1048576 | tf_op jit(solution)/shard_map/reshape | solution.py:467
  24.3 2.2 %collective-permute-start.10 = (f32[20,32,128]{2,1,0:T(8,128)S(1)}, f32[20,32,128]{2,1,0:T(8,128)S(1)}, u32[]{:S(2)}, u32[]{:S(2)}) collective-permute-start(f32[20,32,128]{2,1,0:T(8,128)S(1)} %bitcast.74), channel_id=1, source_target_pairs={{0,24},{2,26},{4,28},{6,30},{8,0},{10,2},{12,4},{14,6},{16,8},{18,... | collective-permute-start | bytes 983048 | tf_op jit(solution)/shard_map/ppermute | solution.py:413
  29.2 5.2 %collective-permute-done.10.refs_25_ = f32[20,32,128]{2,1,0:T(8,128)S(1)} collective-permute-done((f32[20,32,128]{2,1,0:T(8,128)S(1)}, f32[20,32,128]{2,1,0:T(8,128)S(1)}, u32[]{:S(2)}, u32[]{:S(2)}) %collective-permute-start.10) | collective-permute-done | bytes 327712 | tf_op jit(solution)/shard_map/ppermute | solution.py:413
  34.4 2.0 %collective-permute-done.7.refs_19_ = f32[20,32,128]{2,1,0:T(8,128)S(1)} collective-permute-done((f32[20,32,128]{2,1,0:T(8,128)S(1)}, f32[20,32,128]{2,1,0:T(8,128)S(1)}, u32[]{:S(2)}, u32[]{:S(2)}) %collective-permute-start.7) | collective-permute-done | bytes 327712 | tf_op jit(solution)/shard_map/ppermute | solution.py:413
  39.6 7.6 %collective-permute-done.11 = f32[20,32,128]{2,1,0:T(8,128)S(1)} collective-permute-done((f32[20,32,128]{2,1,0:T(8,128)S(1)}, f32[20,32,128]{2,1,0:T(8,128)S(1)}, u32[]{:S(2)}, u32[]{:S(2)}) %collective-permute-start.11) | collective-permute-done | bytes 327712 | tf_op jit(solution)/shard_map/ppermute | solution.py:421
  47.3 1.8 %collective-permute-start.14 = (f32[20,32,128]{2,1,0:T(8,128)S(1)}, f32[20,32,128]{2,1,0:T(8,128)S(1)}, u32[]{:S(2)}, u32[]{:S(2)}) collective-permute-start(f32[20,32,128]{2,1,0:T(8,128)S(1)} %add.128.refs_21_), channel_id=1, source_target_pairs={{0,4},{2,6},{4,0},{6,2},{8,12},{10,14},{12,8},{14,10},{16,20},{18,... | collective-permute-start | bytes 983048 | tf_op jit(solution)/shard_map/ppermute | solution.py:413
  51.8 3.4 %collective-permute-done.14.refs_23_ = f32[20,32,128]{2,1,0:T(8,128)S(1)} collective-permute-done((f32[20,32,128]{2,1,0:T(8,128)S(1)}, f32[20,32,128]{2,1,0:T(8,128)S(1)}, u32[]{:S(2)}, u32[]{:S(2)}) %collective-permute-start.14) | collective-permute-done | bytes 327712 | tf_op jit(solution)/shard_map/ppermute | solution.py:413
  56.8 20.0 %windows.1 = (f32[2,20,32,128]{3,2,1,0:T(8,128)}, f32[2,20,32,128]{3,2,1,0:T(8,128)}, f32[2,20,32,128]{3,2,1,0:T(8,128)}, f32[2,20,32,128]{3,2,1,0:T(8,128)}, f3...) custom-call(s32[6]{0:T(128)S(1)} %gather_fusion, ...), custom_call_target="tpu_custom_call" | custom-call | tf_op jit(solution)/shard_map/windows/pallas_call | solution.py:361
  76.8 16.9 %collective-permute-start.21 = (f32[2,20,32,128]{3,2,1,0:T(8,128)}, f32[2,20,32,128]{3,2,1,0:T(8,128)S(1)}, u32[]{:S(2)}, u32[]{:S(2)}) collective-permute-start(f32[2,20,32,128]{3,2,1,0:T(8,128)} %get-tuple-element.41), channel_id=1, source_target_pairs={{0,2},{2,0},{4,6},{6,4},{8,10},{10,8},{12,14},{14,12},{16,18},{18,... | collective-permute-start | bytes 1966088 | tf_op jit(solution)/shard_map/ppermute | solution.py:413
  96.9 8.0 %collective-permute-start.22 = (f32[20,32,128]{2,1,0:T(8,128)S(1)}, f32[20,32,128]{2,1,0:T(8,128)S(1)}, u32[]{:S(2)}, u32[]{:S(2)}) collective-permute-start(f32[20,32,128]{2,1,0:T(8,128)S(1)} %slice_bitcast_fusion.3), channel_id=1, source_target_pairs={{0,4},{2,6},{4,0},{6,2},{8,12},{10,14},{12,8},{14,10},{16,20},{18,... | collective-permute-start | bytes 983048 | tf_op jit(solution)/shard_map/ppermute | solution.py:413
  105.3 7.9 %collective-permute-done.22 = f32[20,32,128]{2,1,0:T(8,128)S(1)} collective-permute-done((f32[20,32,128]{2,1,0:T(8,128)S(1)}, f32[20,32,128]{2,1,0:T(8,128)S(1)}, u32[]{:S(2)}, u32[]{:S(2)}) %collective-permute-start.22) | collective-permute-done | bytes 327712 | tf_op jit(solution)/shard_map/ppermute | solution.py:413
  113.2 1.7 %collective-permute-start.23 = (f32[20,32,128]{2,1,0:T(8,128)S(1)}, f32[20,32,128]{2,1,0:T(8,128)S(1)}, u32[]{:S(2)}, u32[]{:S(2)}) collective-permute-start(f32[20,32,128]{2,1,0:T(8,128)S(1)} %slice_bitcast_fusion.4), channel_id=1, source_target_pairs={{0,4},{2,6},{4,0},{6,2},{8,12},{10,14},{12,8},{14,10},{16,20},{18,... | collective-permute-start | bytes 983048 | tf_op jit(solution)/shard_map/ppermute | solution.py:413
  117.1 5.5 %collective-permute-done.23 = f32[20,32,128]{2,1,0:T(8,128)S(1)} collective-permute-done((f32[20,32,128]{2,1,0:T(8,128)S(1)}, f32[20,32,128]{2,1,0:T(8,128)S(1)}, u32[]{:S(2)}, u32[]{:S(2)}) %collective-permute-start.23) | collective-permute-done | bytes 327712 | tf_op jit(solution)/shard_map/ppermute | solution.py:413
  124.2 6.9 %collective-permute-done.24 = f32[20,32,128]{2,1,0:T(8,128)S(1)} collective-permute-done((f32[20,32,128]{2,1,0:T(8,128)S(1)}, f32[20,32,128]{2,1,0:T(8,128)S(1)}, u32[]{:S(2)}, u32[]{:S(2)}) %collective-permute-start.24) | collective-permute-done | bytes 327712 | tf_op jit(solution)/shard_map/ppermute | solution.py:413
  133.4 5.4 %collective-permute-done.25 = f32[20,32,128]{2,1,0:T(8,128)S(1)} collective-permute-done((f32[20,32,128]{2,1,0:T(8,128)S(1)}, f32[20,32,128]{2,1,0:T(8,128)S(1)}, u32[]{:S(2)}, u32[]{:S(2)}) %collective-permute-start.25) | collective-permute-done | bytes 327712 | tf_op jit(solution)/shard_map/ppermute | solution.py:413
  138.9 2.5 %collective-permute-done.27 = f32[20,32,128]{2,1,0:T(8,128)S(1)} collective-permute-done((f32[20,32,128]{2,1,0:T(8,128)S(1)}, f32[20,32,128]{2,1,0:T(8,128)S(1)}, u32[]{:S(2)}, u32[]{:S(2)}) %collective-permute-start.27) | collective-permute-done | bytes 327712 | tf_op jit(solution)/shard_map/ppermute | solution.py:413
  142.7 4.5 %collective-permute-start.30 = (f32[2,64,128]{2,1,0:T(8,128)S(1)}, f32[2,64,128]{2,1,0:T(8,128)S(1)}, u32[]{:S(2)}, u32[]{:S(2)}) collective-permute-start(f32[2,64,128]{2,1,0:T(8,128)S(1)} %fusion.28), channel_id=1, source_target_pairs={{0,1},{2,3},{4,5},{6,7},{8,9},{10,11},{12,13},{14,15},{16,17},{18,... | collective-permute-start | bytes 196616 | tf_op jit(solution)/shard_map/ppermute | solution.py:500
  147.6 1.6 %collective-permute-done.30.refs_3_ = f32[2,64,128]{2,1,0:T(8,128)S(1)} collective-permute-done((f32[2,64,128]{2,1,0:T(8,128)S(1)}, f32[2,64,128]{2,1,0:T(8,128)S(1)}, u32[]{:S(2)}, u32[]{:S(2)}) %collective-permute-start.30) | collective-permute-done | bytes 65568 | tf_op jit(solution)/shard_map/ppermute | solution.py:500
  149.8 2.3 %weave.1 = f32[64,1024]{1,0:T(8,128)} custom-call(f32[2,5,64,128]{3,2,1,0:T(8,128)} %bitcast.81, f32[2,5,64,128]{3,2,1,0:T(8,128)} %bitcast.86, f32[2,5,64,128]{3,2,1,0:T(8,128)} %bitcast.84, f32[2,64,128]{2,1,0:T(8,128)} %copy-done.8, f32[2,64,128]{2,1,0:T(8,128)} %copy-done.7), custom_call_target="tpu_custom_call" | custom-call | tf_op jit(solution)/shard_map/weave/pallas_call | solution.py:119
  (102 shorter events, 29.3 us)
Async XLA Ops:
  0.8 6.9 %collective-permute-start.1 = (f32[64,128]{1,0:T(8,128)S(1)}, f32[64,128]{1,0:T(8,128)S(1)}, u32[]{:S(2)}, u32[]{:S(2)}) collective-permute-start(f32[64,128]{1,0:T(8,128)S(1)} %get-tuple-element.45), channel_id=1, source_target_pairs={{0,1},{2,3},{4,5},{6,7},{8,9},{10,11},{12,13},{14,15},{16,17},{18,... | collective-permute-start | bytes 98312 | tf_op jit(solution)/shard_map/ppermute | solution.py:427
  14.3 10.1 %collective-permute-start.5 = (f32[20,32,128]{2,1,0:T(8,128)}, f32[20,32,128]{2,1,0:T(8,128)S(1)}, u32[]{:S(2)}, u32[]{:S(2)}) collective-permute-start(f32[20,32,128]{2,1,0:T(8,128)} %bitcast.71), channel_id=1, source_target_pairs={{0,8},{2,10},{4,12},{6,14},{8,16},{10,18},{12,20},{14,22},{16,24},... | collective-permute-start | bytes 983048 | tf_op jit(solution)/shard_map/ppermute | solution.py:413
  15.8 10.7 %collective-permute-start.3 = (f32[20,32,128]{2,1,0:T(8,128)}, f32[20,32,128]{2,1,0:T(8,128)S(1)}, u32[]{:S(2)}, u32[]{:S(2)}) collective-permute-start(f32[20,32,128]{2,1,0:T(8,128)} %bitcast.72), channel_id=1, source_target_pairs={{0,4},{2,6},{4,0},{6,2},{8,12},{10,14},{12,8},{14,10},{16,20},{18,... | collective-permute-start | bytes 983048 | tf_op jit(solution)/shard_map/ppermute | solution.py:413
  17.4 33.4 %collective-permute-start.2 = (f32[20,32,128]{2,1,0:T(8,128)}, f32[20,32,128]{2,1,0:T(8,128)S(1)}, u32[]{:S(2)}, u32[]{:S(2)}) collective-permute-start(f32[20,32,128]{2,1,0:T(8,128)} %bitcast.73), channel_id=1, source_target_pairs={{0,2},{2,0},{4,6},{6,4},{8,10},{10,8},{12,14},{14,12},{16,18},{18,... | collective-permute-start | bytes 983048 | tf_op jit(solution)/shard_map/ppermute | solution.py:413
  24.3 10.0 %collective-permute-start.10 = (f32[20,32,128]{2,1,0:T(8,128)S(1)}, f32[20,32,128]{2,1,0:T(8,128)S(1)}, u32[]{:S(2)}, u32[]{:S(2)}) collective-permute-start(f32[20,32,128]{2,1,0:T(8,128)S(1)} %bitcast.74), channel_id=1, source_target_pairs={{0,24},{2,26},{4,28},{6,30},{8,0},{10,2},{12,4},{14,6},{16,8},{18,... | collective-permute-start | bytes 983048 | tf_op jit(solution)/shard_map/ppermute | solution.py:413
  26.5 9.8 %collective-permute-start.7 = (f32[20,32,128]{2,1,0:T(8,128)S(1)}, f32[20,32,128]{2,1,0:T(8,128)S(1)}, u32[]{:S(2)}, u32[]{:S(2)}) collective-permute-start(f32[20,32,128]{2,1,0:T(8,128)S(1)} %collective-permute-done.5.refs_17_), channel_id=1, source_target_pairs={{0,4},{2,6},{4,0},{6,2},{8,12},{10,14},{12,8},{14,10},{16,20},{18,... | collective-permute-start | bytes 983048 | tf_op jit(solution)/shard_map/ppermute | solution.py:413
  28.5 10.6 %collective-permute-start.9 = (f32[20,32,128]{2,1,0:T(8,128)S(1)}, f32[20,32,128]{2,1,0:T(8,128)S(1)}, u32[]{:S(2)}, u32[]{:S(2)}) collective-permute-start(f32[20,32,128]{2,1,0:T(8,128)S(1)} %collective-permute-done.5.refs_17_), channel_id=1, source_target_pairs={{8,16},{10,18},{12,20},{14,22},{16,24},{18,26},{20,28},{22,30},{9,... | collective-permute-start | bytes 983048 | tf_op jit(solution)/shard_map/ppermute | solution.py:421
  36.3 10.9 %collective-permute-start.13 = (f32[20,32,128]{2,1,0:T(8,128)S(1)}, f32[20,32,128]{2,1,0:T(8,128)S(1)}, u32[]{:S(2)}, u32[]{:S(2)}) collective-permute-start(f32[20,32,128]{2,1,0:T(8,128)S(1)} %collective-permute-done.10.refs_25_), channel_id=1, source_target_pairs={{0,4},{2,6},{4,0},{6,2},{8,12},{10,14},{12,8},{14,10},{16,20},{18,... | collective-permute-start | bytes 983048 | tf_op jit(solution)/shard_map/ppermute | solution.py:413
  36.9 10.4 %collective-permute-start.11 = (f32[20,32,128]{2,1,0:T(8,128)S(1)}, f32[20,32,128]{2,1,0:T(8,128)S(1)}, u32[]{:S(2)}, u32[]{:S(2)}) collective-permute-start(f32[20,32,128]{2,1,0:T(8,128)S(1)} %collective-permute-done.10.refs_25_), channel_id=1, source_target_pairs={{8,0},{10,2},{12,4},{14,6},{16,8},{18,10},{20,12},{22,14},{9,1},{1... | collective-permute-start | bytes 983048 | tf_op jit(solution)/shard_map/ppermute | solution.py:421
  39.0 12.3 %collective-permute-start.6 = (f32[20,32,128]{2,1,0:T(8,128)S(1)}, f32[20,32,128]{2,1,0:T(8,128)S(1)}, u32[]{:S(2)}, u32[]{:S(2)}) collective-permute-start(f32[20,32,128]{2,1,0:T(8,128)S(1)} %collective-permute-done.5.refs_17_), channel_id=1, source_target_pairs={{0,2},{2,0},{4,6},{6,4},{8,10},{10,8},{12,14},{14,12},{16,18},{18,... | collective-permute-start | bytes 983048 | tf_op jit(solution)/shard_map/ppermute | solution.py:413
  39.1 12.3 %collective-permute-start.4 = (f32[20,32,128]{2,1,0:T(8,128)S(1)}, f32[20,32,128]{2,1,0:T(8,128)S(1)}, u32[]{:S(2)}, u32[]{:S(2)}) collective-permute-start(f32[20,32,128]{2,1,0:T(8,128)S(1)} %collective-permute-done.3.refs_15_), channel_id=1, source_target_pairs={{0,2},{2,0},{4,6},{6,4},{8,10},{10,8},{12,14},{14,12},{16,18},{18,... | collective-permute-start | bytes 983048 | tf_op jit(solution)/shard_map/ppermute | solution.py:413
  47.3 7.9 %collective-permute-start.14 = (f32[20,32,128]{2,1,0:T(8,128)S(1)}, f32[20,32,128]{2,1,0:T(8,128)S(1)}, u32[]{:S(2)}, u32[]{:S(2)}) collective-permute-start(f32[20,32,128]{2,1,0:T(8,128)S(1)} %add.128.refs_21_), channel_id=1, source_target_pairs={{0,4},{2,6},{4,0},{6,2},{8,12},{10,14},{12,8},{14,10},{16,20},{18,... | collective-permute-start | bytes 983048 | tf_op jit(solution)/shard_map/ppermute | solution.py:413
  76.8 18.9 %collective-permute-start.21 = (f32[2,20,32,128]{3,2,1,0:T(8,128)}, f32[2,20,32,128]{3,2,1,0:T(8,128)S(1)}, u32[]{:S(2)}, u32[]{:S(2)}) collective-permute-start(f32[2,20,32,128]{3,2,1,0:T(8,128)} %get-tuple-element.41), channel_id=1, source_target_pairs={{0,2},{2,0},{4,6},{6,4},{8,10},{10,8},{12,14},{14,12},{16,18},{18,... | collective-permute-start | bytes 1966088 | tf_op jit(solution)/shard_map/ppermute | solution.py:413
  93.7 11.3 %collective-permute-start.19 = (f32[2,20,32,128]{3,2,1,0:T(8,128)}, f32[2,20,32,128]{3,2,1,0:T(8,128)S(1)}, u32[]{:S(2)}, u32[]{:S(2)}) collective-permute-start(f32[2,20,32,128]{3,2,1,0:T(8,128)} %get-tuple-element.37), channel_id=1, source_target_pairs={{0,2},{2,0},{4,6},{6,4},{8,10},{10,8},{12,14},{14,12},{16,18},{18,... | collective-permute-start | bytes 1966088 | tf_op jit(solution)/shard_map/ppermute | solution.py:413
  93.8 11.3 %collective-permute-start.20 = (f32[2,20,32,128]{3,2,1,0:T(8,128)}, f32[2,20,32,128]{3,2,1,0:T(8,128)S(1)}, u32[]{:S(2)}, u32[]{:S(2)}) collective-permute-start(f32[2,20,32,128]{3,2,1,0:T(8,128)} %get-tuple-element.39), channel_id=1, source_target_pairs={{0,2},{2,0},{4,6},{6,4},{8,10},{10,8},{12,14},{14,12},{16,18},{18,... | collective-permute-start | bytes 1966088 | tf_op jit(solution)/shard_map/ppermute | solution.py:413
  96.9 16.3 %collective-permute-start.22 = (f32[20,32,128]{2,1,0:T(8,128)S(1)}, f32[20,32,128]{2,1,0:T(8,128)S(1)}, u32[]{:S(2)}, u32[]{:S(2)}) collective-permute-start(f32[20,32,128]{2,1,0:T(8,128)S(1)} %slice_bitcast_fusion.3), channel_id=1, source_target_pairs={{0,4},{2,6},{4,0},{6,2},{8,12},{10,14},{12,8},{14,10},{16,20},{18,... | collective-permute-start | bytes 983048 | tf_op jit(solution)/shard_map/ppermute | solution.py:413
  104.9 10.8 %collective-permute-start.18 = (f32[2,20,32,128]{3,2,1,0:T(8,128)S(1)}, f32[2,20,32,128]{3,2,1,0:T(8,128)S(1)}, u32[]{:S(2)}, u32[]{:S(2)}) collective-permute-start(f32[2,20,32,128]{3,2,1,0:T(8,128)S(1)} %copy-done.11), channel_id=1, source_target_pairs={{0,2},{2,0},{4,6},{6,4},{8,10},{10,8},{12,14},{14,12},{16,18},{18,... | collective-permute-start | bytes 1966088 | tf_op jit(solution)/shard_map/ppermute | solution.py:413
  113.2 9.4 %collective-permute-start.23 = (f32[20,32,128]{2,1,0:T(8,128)S(1)}, f32[20,32,128]{2,1,0:T(8,128)S(1)}, u32[]{:S(2)}, u32[]{:S(2)}) collective-permute-start(f32[20,32,128]{2,1,0:T(8,128)S(1)} %slice_bitcast_fusion.4), channel_id=1, source_target_pairs={{0,4},{2,6},{4,0},{6,2},{8,12},{10,14},{12,8},{14,10},{16,20},{18,... | collective-permute-start | bytes 983048 | tf_op jit(solution)/shard_map/ppermute | solution.py:413
  115.0 9.1 %collective-permute-start.28 = (f32[20,32,128]{2,1,0:T(8,128)S(1)}, f32[20,32,128]{2,1,0:T(8,128)S(1)}, u32[]{:S(2)}, u32[]{:S(2)}) collective-permute-start(f32[20,32,128]{2,1,0:T(8,128)S(1)} %fusion.2), channel_id=1, source_target_pairs={{16,8},{18,10},{20,12},{22,14},{24,16},{26,18},{28,20},{30,22},{17... | collective-permute-start | bytes 983048 | tf_op jit(solution)/shard_map/ppermute | solution.py:421
  115.8 16.5 %collective-permute-start.26 = (f32[20,32,128]{2,1,0:T(8,128)S(1)}, f32[20,32,128]{2,1,0:T(8,128)S(1)}, u32[]{:S(2)}, u32[]{:S(2)}) collective-permute-start(f32[20,32,128]{2,1,0:T(8,128)S(1)} %fusion.2), channel_id=1, source_target_pairs={{0,8},{2,10},{4,12},{6,14},{8,16},{10,18},{12,20},{14,22},{1,9},{3... | collective-permute-start | bytes 983048 | tf_op jit(solution)/shard_map/ppermute | solution.py:421
  122.6 8.6 %collective-permute-start.24 = (f32[20,32,128]{2,1,0:T(8,128)S(1)}, f32[20,32,128]{2,1,0:T(8,128)S(1)}, u32[]{:S(2)}, u32[]{:S(2)}) collective-permute-start(f32[20,32,128]{2,1,0:T(8,128)S(1)} %slice_bitcast_fusion.5), channel_id=1, source_target_pairs={{0,4},{2,6},{4,0},{6,2},{8,12},{10,14},{12,8},{14,10},{16,20},{18,... | collective-permute-start | bytes 983048 | tf_op jit(solution)/shard_map/ppermute | solution.py:413
  124.2 14.7 %collective-permute-start.29 = (f32[20,32,128]{2,1,0:T(8,128)S(1)}, f32[20,32,128]{2,1,0:T(8,128)S(1)}, u32[]{:S(2)}, u32[]{:S(2)}) collective-permute-start(f32[20,32,128]{2,1,0:T(8,128)S(1)} %fusion.1), channel_id=1, source_target_pairs={{0,24},{2,26},{4,28},{6,30},{8,0},{10,2},{12,4},{14,6},{16,8},{18,... | collective-permute-start | bytes 983048 | tf_op jit(solution)/shard_map/ppermute | solution.py:413
  131.1 7.7 %collective-permute-start.25 = (f32[20,32,128]{2,1,0:T(8,128)S(1)}, f32[20,32,128]{2,1,0:T(8,128)S(1)}, u32[]{:S(2)}, u32[]{:S(2)}) collective-permute-start(f32[20,32,128]{2,1,0:T(8,128)S(1)} %slice_bitcast_fusion.6), channel_id=1, source_target_pairs={{0,4},{2,6},{4,0},{6,2},{8,12},{10,14},{12,8},{14,10},{16,20},{18,... | collective-permute-start | bytes 983048 | tf_op jit(solution)/shard_map/ppermute | solution.py:413
  132.4 9.0 %collective-permute-start.27 = (f32[20,32,128]{2,1,0:T(8,128)S(1)}, f32[20,32,128]{2,1,0:T(8,128)S(1)}, u32[]{:S(2)}, u32[]{:S(2)}) collective-permute-start(f32[20,32,128]{2,1,0:T(8,128)S(1)} %fusion.4), channel_id=1, source_target_pairs={{0,8},{2,10},{4,12},{6,14},{8,16},{10,18},{12,20},{14,22},{16,24},... | collective-permute-start | bytes 983048 | tf_op jit(solution)/shard_map/ppermute | solution.py:413
  (20 other events, 155.5 us)
